TPU v7x, 512 devices: a whole 4x8x8 slice. The times are simulated.
512 devices in a mesh: rep: 16 (over y, core), lab: 32 (over x, z).
Axes of the slice: x: 4, y: 8, z: 8, core: 2. Of those that a mesh axis runs over, the one named last changes fastest.
Arguments:
- queries: bfloat16 [65536, 768], P(('rep', 'lab')), may hold values from -6 to 6
- shortlist: int32 [65536, 8], P(('rep', 'lab')), may hold values from 0 to 255, all different within a row; in each aligned block of 128 rows (0 to 127, 128 to 255, ...) at most 8 rows name the same one
- positive: int32 [65536, 8], P(('rep', 'lab')), may hold values from 0 to 255
- label_weight: bfloat16 [32768, 768], P('lab'), may hold values from -0.21875 to 0.21875
- first_moment: float32 [16, 2048, 768], P('rep', 'lab'), may hold values from -6 to 6
- second_moment: float32 [16, 2048, 768], P('rep', 'lab'), may hold values from 0.5 to 8
Outputs:
- query_grad: float32 [65536, 768], P(('rep', 'lab'))
- new_weight: float32 [32768, 768], P('lab')
- new_first: float32 [16, 2048, 768], P('rep', 'lab')
- new_second: float32 [16, 2048, 768], P('rep', 'lab')
Inputs may be any that keep to these rules, and one draw needn't show every extreme that they name: `shortlist`: the 8 blocks of one query are distinct; among the 128 rows of one device (aligned blocks of rows) no block is named by more than 8 rows, and some block is named by exactly 8.
All inputs are finite; a program needn't handle non-finite values.
Results may differ from a plain program's by a relative error of at most 0.0026.
Values may be sent and summed in bfloat16 or wider, within the bound.
No kernel may reach another device: no remote copies, remote signals or barrier semaphores. Data moves between devices by JAX's collectives and lax.ppermute only.
A program may use at most 64 MiB of HBM per device.

v0:
```python
import jax
import jax.numpy as jnp
from jax import lax
from jax.experimental import pallas as pl
from jax.experimental.pallas import tpu as pltpu
from jax.sharding import Mesh
from jax.sharding import PartitionSpec as P

D = 768
BLOCK = 128
K = 8
CAP = 8
LANES = 128
COLS = D // LANES
N_LAB = 32
N_X = 4
N_Z = 8
Q_DEV = 128
UP = 4
ACROSS = COLS - UP
N_Y = 8
BLK_DEV = 8
SLOTS = BLK_DEV * CAP
CHUNK = COLS * SLOTS
SUB = 64
FAR = N_Y // 2 - 1

beta_first = 0.9
beta_second = 0.999
learn_rate = 0.01
adam_epsilon = 1e-08
step_count = 100.0

bf16 = jnp.bfloat16
f32 = jnp.float32


def before_matrix():
    row = lax.broadcasted_iota(jnp.int32, (LANES, LANES), 0)
    col = lax.broadcasted_iota(jnp.int32, (LANES, LANES), 1)
    return (row < col).astype(f32).astype(bf16)


def slot_select(marks):
    named = marks >= 0.0
    earlier = jnp.dot(named.astype(f32).astype(bf16), before_matrix(), preferred_element_type=f32)
    rank = jnp.where(named, earlier, -1.0)
    slot = lax.broadcasted_iota(jnp.int32, (1, CAP, 1), 1).astype(f32)
    return rank[:, None, :] == slot


def begin_kernel(short_ref, pos_ref, rows_ref, up_ref, across_ref):
    info = jnp.concatenate([short_ref[...], pos_ref[...]], axis=0).astype(f32).astype(bf16)
    for c in range(COLS):
        part = rows_ref[:, c * LANES : (c + 1) * LANES]
        if c < UP:
            for z in range(N_Z):
                up_ref[z, c * Q_DEV : (c + 1) * Q_DEV, :] = part
        else:
            across_ref[(c - UP) * Q_DEV : (c - UP + 1) * Q_DEV, :] = part
    for z in range(N_Z):
        up_ref[z, UP * Q_DEV :, :] = info
    across_ref[ACROSS * Q_DEV :, :] = info


def begin(short_t, pos_t, queries):
    return pl.pallas_call(
        begin_kernel,
        out_shape=(
            jax.ShapeDtypeStruct((N_Z, UP * Q_DEV + 2 * K, LANES), bf16),
            jax.ShapeDtypeStruct((ACROSS * Q_DEV + 2 * K, LANES), bf16),
        ),
        cost_estimate=pl.CostEstimate(flops=0, bytes_accessed=1_500_000, transcendentals=0),
        name="begin",
    )(short_t, pos_t, queries)


def marks_of(block, short, positive):
    marks = jnp.full(block.shape, -1.0, f32)
    for k in range(K):
        marks = jnp.where(block == short[k : k + 1, :], positive[k : k + 1, :], marks)
    return marks


def one_hot(marks):
    return slot_select(marks).astype(f32).reshape(marks.shape[0] * CAP, LANES).astype(bf16)


def across_kernel(where_ref, short_ref, pos_ref, *refs):
    *source_refs, out_ref, pick_ref = refs
    x = where_ref[2]
    nblk = N_LAB * BLK_DEV
    every = lax.broadcasted_iota(jnp.int32, (nblk, LANES), 0).astype(f32)
    short, positive = short_ref[...].astype(f32), pos_ref[...].astype(f32)
    pick_ref[...] = one_hot(marks_of(every, short, positive))
    here = N_Z * BLK_DEV
    block = (lax.broadcasted_iota(jnp.int32, (here, LANES), 0) + x * here).astype(f32)
    marks = []
    for ref in source_refs:
        info = ref[ACROSS * Q_DEV :, :].astype(f32)
        marks.append(marks_of(block, info[:K], info[K:]))
    pick = one_hot(jnp.concatenate(marks, axis=0))
    for t, ref in enumerate(source_refs):
        rows = jnp.concatenate(
            [ref[c * Q_DEV : (c + 1) * Q_DEV, :] for c in range(ACROSS)], axis=1
        )
        chosen = jnp.dot(
            pick[t * here * CAP : (t + 1) * here * CAP], rows, preferred_element_type=f32
        ).astype(bf16)
        for z in range(N_Z):
            for c in range(ACROSS):
                out_ref[z, t, c * SLOTS : (c + 1) * SLOTS, :] = chosen[
                    z * SLOTS : (z + 1) * SLOTS, c * LANES : (c + 1) * LANES
                ]


def select_across(where, short_t, pos_t, sources):
    return pl.pallas_call(
        across_kernel,
        in_specs=[pl.BlockSpec(memory_space=pltpu.SMEM)]
        + [pl.BlockSpec(memory_space=pltpu.VMEM)] * (2 + N_X),
        out_shape=(
            jax.ShapeDtypeStruct((N_Z, N_X, ACROSS * SLOTS, LANES), bf16),
            jax.ShapeDtypeStruct((N_LAB * SLOTS, LANES), bf16),
        ),
        cost_estimate=pl.CostEstimate(flops=200_000_000, bytes_accessed=2_000_000, transcendentals=0),
        name="select_across",
    )(where, short_t, pos_t, *sources)


def up_kernel(where_ref, arrived_ref, *out_refs):
    x, z = where_ref[2], where_ref[3]
    index = lax.broadcasted_iota(jnp.int32, (N_X * BLK_DEV, LANES), 0)
    owner_x = (index // BLK_DEV + x) % N_X
    block = (owner_x * (N_Z * BLK_DEV) + z * BLK_DEV + index % BLK_DEV).astype(f32)
    marks = []
    for s in range(N_Z):
        info = arrived_ref[s, UP * Q_DEV :, :].astype(f32)
        marks.append(marks_of(block, info[:K], info[K:]))
    pick = one_hot(jnp.concatenate(marks, axis=0))
    count = N_X * SLOTS
    for s in range(N_Z):
        rows = jnp.concatenate(
            [arrived_ref[s, c * Q_DEV : (c + 1) * Q_DEV, :] for c in range(UP)], axis=1
        )
        chosen = jnp.dot(
            pick[s * count : (s + 1) * count], rows, preferred_element_type=f32
        ).astype(bf16)
        for t in range(N_X):
            for c in range(UP):
                out_refs[t][s, c * SLOTS : (c + 1) * SLOTS, :] = chosen[
                    t * SLOTS : (t + 1) * SLOTS, c * LANES : (c + 1) * LANES
                ]
            out_refs[t][s, UP * SLOTS :, :] = marks[s][t * BLK_DEV : (t + 1) * BLK_DEV].astype(bf16)


def select_up(where, arrived):
    return pl.pallas_call(
        up_kernel,
        in_specs=[
            pl.BlockSpec(memory_space=pltpu.SMEM),
            pl.BlockSpec(memory_space=pltpu.VMEM),
        ],
        out_shape=tuple(
            jax.ShapeDtypeStruct((N_Z, UP * SLOTS + BLK_DEV, LANES), bf16) for _ in range(N_X)
        ),
        cost_estimate=pl.CostEstimate(flops=300_000_000, bytes_accessed=3_000_000, transcendentals=0),
        name="select_up",
    )(where, arrived)


def block_kernel(
    where_ref, a0_ref, a1_ref, a2_ref, a3_ref, b_ref, tiles_ref, back_ref, keep_ref, give_ref, marks_ref, rows_ref
):
    a_refs = (a0_ref, a1_ref, a2_ref, a3_ref)
    x = where_ref[2]
    pair = pl.program_id(0)
    y, core = where_ref[0], where_ref[1]

    @pl.when(pair == 0)
    def _():
        for t in range(N_X):
            marks = a_refs[t][:, UP * SLOTS :, :].astype(f32)
            for b in range(BLK_DEV):
                marks_ref[b, t * N_Z : (t + 1) * N_Z, :] = marks[:, b, :]

    for c in range(COLS):
        group = c if c < UP else c - UP
        at = pl.ds(pl.multiple_of(group * SLOTS + pair * 2 * CAP, 2 * CAP), 2 * CAP)
        for t in range(N_X):
            part = a_refs[t][:, at, :] if c < UP else b_ref[:, t, at, :]
            both = part.astype(f32).reshape(N_Z, 2, CAP, LANES)
            for h in range(2):
                rows_ref[h, t * SLOTS : (t + 1) * SLOTS, c * LANES : (c + 1) * LANES] = (
                    both[:, h].reshape(N_Z * CAP, LANES).astype(bf16)
                )

    label = lax.broadcasted_iota(jnp.int32, (N_LAB * CAP, BLOCK), 1).astype(f32)
    parts = []
    for h in range(2):
        marks = marks_ref[pair * 2 + h]
        held = jnp.where(slot_select(marks), marks[:, None, :] + 1.0, 0.0)
        mark = (jnp.sum(held, axis=2, keepdims=True) - 1.0).reshape(N_LAB * CAP, 1)
        rows = rows_ref[h]
        tile = tiles_ref[h * BLOCK : (h + 1) * BLOCK, :]
        logits = lax.dot_general(rows, tile, (((1,), (1,)), ((), ())), preferred_element_type=f32)
        slopes = (jax.nn.sigmoid(logits) - (label == mark).astype(f32)).astype(bf16)
        parts.append(jnp.dot(slopes, tile, preferred_element_type=f32))
        grad = lax.dot_general(slopes, rows, (((0,), (0,)), ((), ())), preferred_element_type=f32)
        ahead = lax.rem(pair * 2 + h - y + N_Y, N_Y)
        halved = lax.rem(ahead, N_Y // 2) == 0
        first = ahead < N_Y // 2
        unit = jnp.where(first, ahead, N_Y - ahead) * 2 - 2
        own = jnp.where(first, 0, 1) == core
        for i in range(2):
            at = jnp.where(halved, jnp.where(first, N_Y - 1, N_Y - 2), unit + i)
            kept = jnp.where(halved, core == i, own)

            @pl.when(kept)
            def _():
                keep_ref[at] = grad[i * SUB : (i + 1) * SUB]

            @pl.when(jnp.logical_not(kept))
            def _():
                give_ref[at] = grad[i * SUB : (i + 1) * SUB]

    for c in range(COLS):
        at = pl.ds(pl.multiple_of(c * SLOTS + pair * 2 * CAP, 2 * CAP), 2 * CAP)
        cols = slice(c * LANES, (c + 1) * LANES)
        both = jnp.stack([p[:, cols].reshape(N_LAB, CAP, LANES) for p in parts], axis=1)
        both = both.reshape(N_LAB, 2 * CAP, LANES).astype(bf16)
        for t in range(N_X):
            source_x = lax.rem(x - t + N_X, N_X)
            back_ref[pl.ds(source_x * N_Z, N_Z), at, :] = both[t * N_Z : (t + 1) * N_Z]


def label_blocks(where, up, across, label_weight):
    pairs = BLK_DEV // 2
    return pl.pallas_call(
        block_kernel,
        grid=(pairs,),
        in_specs=[
            pl.BlockSpec(memory_space=pltpu.SMEM),
        ]
        + [pl.BlockSpec((N_Z, UP * SLOTS + BLK_DEV, LANES), lambda p: (0, 0, 0))] * N_X
        + [
            pl.BlockSpec((N_Z, N_X, ACROSS * SLOTS, LANES), lambda p: (0, 0, 0, 0)),
            pl.BlockSpec((2 * BLOCK, D), lambda p: (p, 0)),
        ],
        out_specs=[
            pl.BlockSpec((N_LAB, CHUNK, LANES), lambda p: (0, 0, 0)),
            pl.BlockSpec((N_Y, SUB, D), lambda p: (0, 0, 0)),
            pl.BlockSpec((N_Y, SUB, D), lambda p: (0, 0, 0)),
        ],
        out_shape=(
            jax.ShapeDtypeStruct((N_LAB, CHUNK, LANES), bf16),
            jax.ShapeDtypeStruct((BLK_DEV, SUB, D), f32),
            jax.ShapeDtypeStruct((BLK_DEV, SUB, D), f32),
        ),
        scratch_shapes=[
            pltpu.VMEM((BLK_DEV, N_LAB, LANES), f32),
            pltpu.VMEM((2, N_LAB * CAP, D), bf16),
        ],
        cost_estimate=pl.CostEstimate(
            flops=1_210_000_000, bytes_accessed=11_000_000, transcendentals=300_000
        ),
        name="label_blocks",
    )(where, *up, across, label_weight)


def sum_kernel(pick_ref, back_ref, out_ref):
    step = pl.program_id(0)
    groups = back_ref.shape[0]
    pick = pick_ref[...]
    cols = []
    for c in range(COLS):
        part = back_ref[:, c * SLOTS : (c + 1) * SLOTS, :].reshape(groups * SLOTS, LANES)
        cols.append(part)
    parts = jnp.concatenate(cols, axis=1)
    total = lax.dot_general(pick, parts, (((0,), (0,)), ((), ())), preferred_element_type=f32)

    @pl.when(step == 0)
    def _():
        out_ref[...] = total

    @pl.when(step > 0)
    def _():
        out_ref[...] += total


def sum_parts(pick, back):
    steps = 4
    groups = N_LAB // steps
    return pl.pallas_call(
        sum_kernel,
        grid=(steps,),
        in_specs=[
            pl.BlockSpec((groups * SLOTS, LANES), lambda g: (g, 0)),
            pl.BlockSpec((groups, CHUNK, LANES), lambda g: (g, 0, 0)),
        ],
        out_specs=pl.BlockSpec((LANES, D), lambda g: (0, 0)),
        out_shape=jax.ShapeDtypeStruct((LANES, D), f32),
        cost_estimate=pl.CostEstimate(flops=400_000_000, bytes_accessed=4_000_000, transcendentals=0),
        name="sum_parts",
    )(pick, back)


def split_kernel(keep_ref, got_ref, *out_refs):
    for s in range(FAR):
        for i in range(2):
            u = 2 * s + i
            out_refs[s][i * SUB : (i + 1) * SUB, :] = (keep_ref[u] + got_ref[u]).astype(bf16)
    out_refs[FAR][...] = (keep_ref[2 * FAR] + got_ref[2 * FAR]).astype(bf16)
    out_refs[FAR + 1][...] = keep_ref[2 * FAR + 1] + got_ref[2 * FAR + 1]


def split_by_y(keep, got):
    return pl.pallas_call(
        split_kernel,
        out_shape=tuple(jax.ShapeDtypeStruct((BLOCK, D), bf16) for _ in range(FAR))
        + (jax.ShapeDtypeStruct((SUB, D), bf16), jax.ShapeDtypeStruct((SUB, D), f32)),
        cost_estimate=pl.CostEstimate(flops=400_000, bytes_accessed=4_000_000, transcendentals=0),
        name="split_by_y",
    )(keep, got)


def weight_block(tile_ref, out_ref, step):
    out_ref[...] = tile_ref[...].astype(f32) - learn_rate * step.astype(f32)


def near_kernel(where_ref, tile_ref, both_ref, one_ref, two_ref, three_ref, out_ref):
    step = pl.program_id(0)
    for i, ref in enumerate((both_ref, one_ref, two_ref, three_ref)):

        @pl.when(step == i)
        def _():
            weight_block(tile_ref, out_ref, ref[...])


def far_kernel(where_ref, tile_ref, mine_ref, other_ref, begun_ref, out_ref):
    step = pl.program_id(0)
    core = where_ref[1]

    @pl.when(step == 0)
    def _():
        mine = mine_ref[...].astype(f32)
        other = other_ref[FAR * BLOCK :, :].astype(f32)
        low = jnp.where(core == 0, mine, other)
        high = jnp.where(core == 0, other, mine)
        weight_block(tile_ref, out_ref, jnp.concatenate([low, high], axis=0))

    for i in range(FAR):

        @pl.when(step == i + 1)
        def _():
            weight_block(tile_ref, out_ref, other_ref[i * BLOCK : (i + 1) * BLOCK, :])


def way(where_ref):
    return 1 - 2 * where_ref[1]


def near_tile(t, where_ref):
    return (lax.rem(where_ref[0] - way(where_ref) * t + N_Y, N_Y), 0)


def far_tile(t, where_ref):
    ahead = jnp.where(t == 0, N_Y // 2, way(where_ref) * t)
    return (lax.rem(where_ref[0] + ahead + N_Y, N_Y), 0)


def whole(shape):
    return pl.BlockSpec(shape, lambda t, where_ref: (0,) * len(shape))


def fresh_weight(where, label_weight, both, near, opposite, other):
    out_shape = jax.ShapeDtypeStruct((N_Y * BLOCK, D), f32)
    cost = pl.CostEstimate(flops=800_000, bytes_accessed=3_200_000, transcendentals=0)
    begun = pl.pallas_call(
        near_kernel,
        grid_spec=pltpu.PrefetchScalarGridSpec(
            num_scalar_prefetch=1,
            grid=(N_Y // 2,),
            in_specs=[pl.BlockSpec((BLOCK, D), near_tile)] + [whole((BLOCK, D))] * 4,
            out_specs=pl.BlockSpec((BLOCK, D), near_tile),
        ),
        out_shape=out_shape,
        cost_estimate=cost,
        name="near_weight",
    )(where, label_weight, both, *near)
    return pl.pallas_call(
        far_kernel,
        grid_spec=pltpu.PrefetchScalarGridSpec(
            num_scalar_prefetch=1,
            grid=(N_Y // 2,),
            in_specs=[
                pl.BlockSpec((BLOCK, D), far_tile),
                whole((SUB, D)),
                whole((FAR * BLOCK + SUB, D)),
                pl.BlockSpec(memory_space=pl.ANY),
            ],
            out_specs=pl.BlockSpec((BLOCK, D), far_tile),
        ),
        out_shape=out_shape,
        input_output_aliases={4: 0},
        cost_estimate=cost,
        name="far_weight",
    )(where, label_weight, opposite, other, begun)


def along_y(shift):
    return [(y * 2 + c, ((y + (1 - 2 * c) * shift) % N_Y) * 2 + c) for y in range(N_Y) for c in range(2)]


OTHER_CORE = [(r, r ^ 1) for r in range(2 * N_Y)]


def along_x(shift):
    return [(x, (x + shift) % N_X) for x in range(N_X)]


def body(queries, shortlist, positive, label_weight, first_moment, second_moment):
    rep = lax.axis_index("rep")
    where = jnp.stack([rep // 2, rep % 2, lax.axis_index("x"), lax.axis_index("z")])
    where = where.astype(jnp.int32)
    short_t, pos_t = shortlist.T, positive.T
    up, across = begin(short_t, pos_t, queries)
    up = lax.all_to_all(up, "z", split_axis=0, concat_axis=0, tiled=True)
    sources = [across] + [lax.ppermute(across, "x", along_x(t)) for t in range(1, N_X)]
    across, pick = select_across(where, short_t, pos_t, sources)
    across = lax.all_to_all(across, "z", split_axis=0, concat_axis=0, tiled=True)
    up = select_up(where, up)
    up = [up[0]] + [lax.ppermute(up[t], "x", along_x(t)) for t in range(1, N_X)]
    back, keep, give = label_blocks(where, up, across, label_weight)
    returned = lax.all_to_all(back, ("x", "z"), split_axis=0, concat_axis=0, tiled=True)

    got = lax.ppermute(give, "rep", OTHER_CORE)
    *sides, opposite, grad = split_by_y(keep, got)
    side = jnp.zeros((BLOCK, D), f32)
    for i, share in enumerate(sides):
        side = side + lax.ppermute(share, "rep", along_y(i + 1)).astype(f32)
    first_core = where[1] == 0
    far = lax.ppermute(opposite, "rep", along_y(N_Y // 2)).astype(f32)
    low = side[:SUB] + jnp.where(first_core, far, 0.0)
    high = side[SUB:] + jnp.where(first_core, 0.0, far)
    grad = grad + jnp.where(first_core, low, high)
    grad = grad + lax.ppermute(jnp.where(first_core, high, low), "rep", OTHER_CORE)
    grad = grad[None]
    new_first = beta_first * first_moment + (1.0 - beta_first) * grad
    new_second = beta_second * second_moment + (1.0 - beta_second) * grad * grad
    first_hat = new_first / (1.0 - beta_first**step_count)
    second_hat = new_second / (1.0 - beta_second**step_count)
    step = (first_hat / (jnp.sqrt(second_hat) + adam_epsilon)).astype(bf16)[0]
    opposite = lax.ppermute(step, "rep", along_y(N_Y // 2))
    theirs = lax.ppermute(step, "rep", OTHER_CORE)
    both = jnp.concatenate(
        [jnp.where(first_core, step, theirs), jnp.where(first_core, theirs, step)], axis=0
    )
    near = [lax.ppermute(both, "rep", along_y(i + 1)) for i in range(FAR)]
    other = lax.ppermute(jnp.concatenate([*near, opposite], axis=0), "rep", OTHER_CORE)
    new_weight = fresh_weight(where, label_weight, both, near, opposite, other)

    query_grad = sum_parts(pick, returned)
    return (query_grad, new_weight, new_first, new_second)


def solution(mesh):
    split = Mesh(
        mesh.devices.reshape(mesh.devices.shape[0], N_X, N_Z), ("rep", "x", "z")
    )
    rows = P(("rep", "x", "z"), None)
    labels = P(("x", "z"), None)
    state = P("rep", ("x", "z"), None)
    return jax.shard_map(
        body,
        mesh=split,
        in_specs=(rows, rows, rows, labels, state, state),
        out_specs=(rows, labels, state, state),
        check_vma=False,
    )
```

profile of v0, /device:TPU:3, one launch (start us, length us, event | category | flops | bytes accessed | tf_op | source)
XLA Modules:
  0.0 193.0 jit_solution(2389487174576048933)
XLA Ops:
  2.7 10.2 %all-to-all-start = ((bf16[8,528,128]{2,1,0:T(8,128)(2,1)}), bf16[8,528,128]{2,1,0:T(8,128)(2,1)S(1)}, u32[]{:S(2)}, u32[]{:S(2)}) async-start(bf16[8,528,128]{2,1,0:T(8,128)(2,1)} %get-tuple-element.22), calls=%async_computation | async-start | bytes 2162688 | tf_op jit(solution)/shard_map/all_to_all | solution.py:428
  15.1 4.0 %collective-permute-start.1 = (bf16[272,128]{1,0:T(8,128)(2,1)S(1)}, bf16[272,128]{1,0:T(8,128)(2,1)S(1)}, u32[]{:S(2)}, u32[]{:S(2)}) collective-permute-start(bf16[272,128]{1,0:T(8,128)(2,1)S(1)} %copy-done.14), channel_id=1, source_target_pairs={{0,16},{8,24},{16,0},{24,8},{1,17},{9,25},{17,1},{25,9},{2,18},{10... | collective-permute-start | bytes 208904 | tf_op jit(solution)/shard_map/ppermute | solution.py:429
  19.1 3.4 %collective-permute-start = (bf16[272,128]{1,0:T(8,128)(2,1)S(1)}, bf16[272,128]{1,0:T(8,128)(2,1)S(1)}, u32[]{:S(2)}, u32[]{:S(2)}) collective-permute-start(bf16[272,128]{1,0:T(8,128)(2,1)S(1)} %copy-done.14), channel_id=1, source_target_pairs={{0,8},{8,16},{16,24},{24,0},{1,9},{9,17},{17,25},{25,1},{2,10},{10... | collective-permute-start | bytes 208904 | tf_op jit(solution)/shard_map/ppermute | solution.py:429
  27.9 14.9 %all-to-all-done.arrived_ref = bf16[8,528,128]{2,1,0:T(8,128)(2,1)S(1)} async-done(((bf16[8,528,128]{2,1,0:T(8,128)(2,1)}), bf16[8,528,128]{2,1,0:T(8,128)(2,1)S(1)}, u32[]{:S(2)}, u32[]{:S(2)}) %all-to-all-start) | async-done | bytes 1081376 | tf_op jit(solution)/shard_map/all_to_all | solution.py:428
  42.8 3.6 %all-to-all-start.1 = ((bf16[8,4,128,128]{3,2,1,0:T(8,128)(2,1)}), bf16[8,4,128,128]{3,2,1,0:T(8,128)(2,1)S(1)}, u32[]{:S(2)}, u32[]{:S(2)}) async-start(bf16[8,4,128,128]{3,2,1,0:T(8,128)(2,1)} %get-tuple-element.27), calls=%async_computation.1 | async-start | bytes 2097152 | tf_op jit(solution)/shard_map/all_to_all | solution.py:431
  46.4 3.3 %select_up.1 = (bf16[8,264,128]{2,1,0:T(8,128)(2,1)}, bf16[8,264,128]{2,1,0:T(8,128)(2,1)}, bf16[8,264,128]{2,1,0:T(8,128)(2,1)}, bf16[8,264,128]{2,1,0:T(8,128)(2,1)}) custom-call(s32[4]{0:T(128)} %pad_add_fusion.where_ref, bf16[8,528,128]{2,1,0:T(8,128)(2,1)} %copy-done.2), custom_call_target="tpu_custom_call" | custom-call | flops 300000000 | bytes 3000000 | tf_op jit(solution)/shard_map/select_up/pallas_call | solution.py:158
  55.6 3.8 %collective-permute-start.5 = (bf16[8,264,128]{2,1,0:T(8,128)(2,1)}, bf16[8,264,128]{2,1,0:T(8,128)(2,1)S(1)}, u32[]{:S(2)}, u32[]{:S(2)}) collective-permute-start(bf16[8,264,128]{2,1,0:T(8,128)(2,1)} %get-tuple-element.26), channel_id=1, source_target_pairs={{0,24},{8,0},{16,8},{24,16},{1,25},{9,1},{17,9},{25,17},{2,26},{10... | collective-permute-start | bytes 1622024 | tf_op jit(solution)/shard_map/ppermute | solution.py:433
  59.4 16.2 %all-to-all-done.1.b_ref = bf16[8,4,128,128]{3,2,1,0:T(8,128)(2,1)S(1)} async-done(((bf16[8,4,128,128]{3,2,1,0:T(8,128)(2,1)}), bf16[8,4,128,128]{3,2,1,0:T(8,128)(2,1)S(1)}, u32[]{:S(2)}, u32[]{:S(2)}) %all-to-all-start.1) | async-done | bytes 1048608 | tf_op jit(solution)/shard_map/all_to_all | solution.py:431
  75.5 6.7 %collective-permute-done.5.a3_ref = bf16[8,264,128]{2,1,0:T(8,128)(2,1)S(1)} collective-permute-done((bf16[8,264,128]{2,1,0:T(8,128)(2,1)}, bf16[8,264,128]{2,1,0:T(8,128)(2,1)S(1)}, u32[]{:S(2)}, u32[]{:S(2)}) %collective-permute-start.5) | collective-permute-done | bytes 540704 | tf_op jit(solution)/shard_map/ppermute | solution.py:433
  83.1 11.0 %label_blocks.1 = (bf16[32,384,128]{2,1,0:T(8,128)(2,1)}, f32[8,64,768]{2,1,0:T(8,128)}, f32[8,64,768]{2,1,0:T(8,128)}) custom-call(s32[4]{0:T(128)} %pad_add_fusion.where_ref, bf16[8,264,128]{2,1,0:T(8,128)(2,1)} %get-tuple-element.23.a0_ref, bf16[8,264,128]{2,1,0:T(8,128)(2,1)} %copy-done.7, bf16[8,264,128]{2,1,0:T(8,128)(2,1)} %copy-done.8, ...), custom_call_target="tpu_custom_call" | custom-call | flops 1210000000 | bytes 11000000 | tf_op jit(solution)/shard_map/label_blocks/pallas_call | solution.py:239
  94.1 8.2 %all-to-all-start.2 = ((bf16[32,384,128]{2,1,0:T(8,128)(2,1)}), bf16[32,384,128]{2,1,0:T(8,128)(2,1)S(1)}, u32[]{:S(2)}, u32[]{:S(2)}) async-start(bf16[32,384,128]{2,1,0:T(8,128)(2,1)} %get-tuple-element.28), calls=%async_computation.2 | async-start | bytes 6291456 | tf_op jit(solution)/shard_map/all_to_all | solution.py:435
  105.6 3.4 %collective-permute-done.6.got_ref = f32[8,64,768]{2,1,0:T(8,128)} collective-permute-done((f32[8,64,768]{2,1,0:T(8,128)}, f32[8,64,768]{2,1,0:T(8,128)}, u32[]{:S(2)}, u32[]{:S(2)}) %collective-permute-start.6) | collective-permute-done | bytes 1572896 | tf_op jit(solution)/shard_map/ppermute | solution.py:437
  111.8 5.2 %collective-permute-start.7 = (bf16[128,768]{1,0:T(8,128)(2,1)}, bf16[128,768]{1,0:T(8,128)(2,1)}, u32[]{:S(2)}, u32[]{:S(2)}) collective-permute-start(bf16[128,768]{1,0:T(8,128)(2,1)} %get-tuple-element.32), channel_id=1, source_target_pairs={{0,64},{32,480},{64,128},{96,32},{128,192},{160,96},{192,256},{224... | collective-permute-start | bytes 589832 | tf_op jit(solution)/shard_map/ppermute | solution.py:441
  117.0 3.8 %collective-permute-start.8 = (bf16[128,768]{1,0:T(8,128)(2,1)}, bf16[128,768]{1,0:T(8,128)(2,1)}, u32[]{:S(2)}, u32[]{:S(2)}) collective-permute-start(bf16[128,768]{1,0:T(8,128)(2,1)} %get-tuple-element.33), channel_id=1, source_target_pairs={{0,128},{32,416},{64,192},{96,480},{128,256},{160,32},{192,320},{2... | collective-permute-start | bytes 589832 | tf_op jit(solution)/shard_map/ppermute | solution.py:441
  123.5 5.8 %collective-permute-start.10 = (bf16[64,768]{1,0:T(8,128)(2,1)}, bf16[64,768]{1,0:T(8,128)(2,1)S(1)}, u32[]{:S(2)}, u32[]{:S(2)}) collective-permute-start(bf16[64,768]{1,0:T(8,128)(2,1)} %get-tuple-element.35), channel_id=1, source_target_pairs={{0,256},{32,288},{64,320},{96,352},{128,384},{160,416},{192,448},{... | collective-permute-start | bytes 294920 | tf_op jit(solution)/shard_map/ppermute | solution.py:443
  131.2 4.3 %collective-permute-done.10 = bf16[64,768]{1,0:T(8,128)(2,1)S(1)} collective-permute-done((bf16[64,768]{1,0:T(8,128)(2,1)}, bf16[64,768]{1,0:T(8,128)(2,1)S(1)}, u32[]{:S(2)}, u32[]{:S(2)}) %collective-permute-start.10) | collective-permute-done | bytes 98336 | tf_op jit(solution)/shard_map/ppermute | solution.py:443
  135.5 6.0 %collective-permute-start.11 = (f32[64,768]{1,0:T(8,128)S(1)}, f32[64,768]{1,0:T(8,128)S(1)}, u32[]{:S(2)}, u32[]{:S(2)}) collective-permute-start(f32[64,768]{1,0:T(8,128)S(1)} %fusion.4), channel_id=1, source_target_pairs={{0,32},{32,0},{64,96},{96,64},{128,160},{160,128},{192,224},{224,1... | collective-permute-start | bytes 589832 | tf_op jit(solution)/shard_map/ppermute | solution.py:447
  146.8 5.0 %collective-permute-start.16 = (bf16[128,768]{1,0:T(8,128)(2,1)S(1)}, bf16[128,768]{1,0:T(8,128)(2,1)S(1)}, u32[]{:S(2)}, u32[]{:S(2)}) collective-permute-start(bf16[128,768]{1,0:T(8,128)(2,1)S(1)} %pad_maximum_fusion.1.both_ref), channel_id=1, source_target_pairs={{0,192},{32,352},{64,256},{96,416},{128,320},{160,480},{192,384},{... | collective-permute-start | bytes 589832 | tf_op jit(solution)/shard_map/ppermute | solution.py:459
  154.0 5.5 %collective-permute-start.14 = (bf16[128,768]{1,0:T(8,128)(2,1)S(1)}, bf16[128,768]{1,0:T(8,128)(2,1)S(1)}, u32[]{:S(2)}, u32[]{:S(2)}) collective-permute-start(bf16[128,768]{1,0:T(8,128)(2,1)S(1)} %pad_maximum_fusion.1.both_ref), channel_id=1, source_target_pairs={{0,64},{32,480},{64,128},{96,32},{128,192},{160,96},{192,256},{224... | collective-permute-start | bytes 589832 | tf_op jit(solution)/shard_map/ppermute | solution.py:459
  159.5 3.9 %collective-permute-start.12 = (bf16[64,768]{1,0:T(8,128)(2,1)S(1)}, bf16[64,768]{1,0:T(8,128)(2,1)S(1)}, u32[]{:S(2)}, u32[]{:S(2)}) collective-permute-start(bf16[64,768]{1,0:T(8,128)(2,1)S(1)} %get-tuple-element.36), channel_id=1, source_target_pairs={{0,256},{32,288},{64,320},{96,352},{128,384},{160,416},{192,448},{... | collective-permute-start | bytes 294920 | tf_op jit(solution)/shard_map/ppermute | solution.py:454
  163.4 9.6 %collective-permute-done.12.mine_ref = bf16[64,768]{1,0:T(8,128)(2,1)S(1)} collective-permute-done((bf16[64,768]{1,0:T(8,128)(2,1)S(1)}, bf16[64,768]{1,0:T(8,128)(2,1)S(1)}, u32[]{:S(2)}, u32[]{:S(2)}) %collective-permute-start.12) | collective-permute-done | bytes 98336 | tf_op jit(solution)/shard_map/ppermute | solution.py:454
  178.1 4.6 %near_weight.1.begun_ref = f32[1024,768]{1,0:T(8,128)} custom-call(s32[4]{0:T(128)} %pad_add_fusion.where_ref, bf16[1024,768]{1,0:T(8,128)(2,1)} %tile_ref.3, bf16[128,768]{1,0:T(8,128)(2,1)} %copy-done.3, bf16[128,768]{1,0:T(8,128)(2,1)} %copy-done.6, bf16[128,768]{1,0:T(8,128)(2,1)} %copy-done.5, bf16[128,768]{1,0:T(8,128)(2,1)} %copy-done.4), custom_call_target="tpu_custom_call" | custom-call | flops 800000 | bytes 3200000 | tf_op jit(solution)/shard_map/near_weight/pallas_call | solution.py:379
  182.6 4.5 %far_weight.1 = f32[1024,768]{1,0:T(8,128)} custom-call(s32[4]{0:T(128)} %pad_add_fusion.where_ref, bf16[1024,768]{1,0:T(8,128)(2,1)} %tile_ref.3, bf16[64,768]{1,0:T(8,128)(2,1)} %copy-done.10, bf16[448,768]{1,0:T(8,128)(2,1)} %collective-permute-done.17.other_ref, f32[1024,768]{1,0:T(8,128)} %near_weight.1.begun_ref), custom_call_target="tpu_custom_call", output_to_operand_aliasing={{}: (4, {})} | custom-call | flops 800000 | bytes 3200000 | tf_op jit(solution)/shard_map/far_weight/pallas_call | solution.py:391
  188.8 4.2 %sum_parts.1 = f32[128,768]{1,0:T(8,128)} custom-call(bf16[2048,128]{1,0:T(8,128)(2,1)} %get-tuple-element.21.pick_ref, bf16[32,384,128]{2,1,0:T(8,128)(2,1)} %copy-done), custom_call_target="tpu_custom_call" | custom-call | flops 400000000 | bytes 4000000 | tf_op jit(solution)/shard_map/sum_parts/pallas_call | solution.py:294
  (69 shorter events, 41.0 us)
Async XLA Ops:
  2.7 40.1 %all-to-all-start = ((bf16[8,528,128]{2,1,0:T(8,128)(2,1)}), bf16[8,528,128]{2,1,0:T(8,128)(2,1)S(1)}, u32[]{:S(2)}, u32[]{:S(2)}) async-start(bf16[8,528,128]{2,1,0:T(8,128)(2,1)} %get-tuple-element.22), calls=%async_computation | async-start | bytes 2162688 | tf_op jit(solution)/shard_map/all_to_all | solution.py:428
  12.9 10.3 %collective-permute-start.2 = (bf16[272,128]{1,0:T(8,128)(2,1)S(1)}, bf16[272,128]{1,0:T(8,128)(2,1)S(1)}, u32[]{:S(2)}, u32[]{:S(2)}) collective-permute-start(bf16[272,128]{1,0:T(8,128)(2,1)S(1)} %copy-done.14), channel_id=1, source_target_pairs={{0,24},{8,0},{16,8},{24,16},{1,25},{9,1},{17,9},{25,17},{2,26},{10... | collective-permute-start | bytes 208904 | tf_op jit(solution)/shard_map/ppermute | solution.py:429
  15.1 8.1 %collective-permute-start.1 = (bf16[272,128]{1,0:T(8,128)(2,1)S(1)}, bf16[272,128]{1,0:T(8,128)(2,1)S(1)}, u32[]{:S(2)}, u32[]{:S(2)}) collective-permute-start(bf16[272,128]{1,0:T(8,128)(2,1)S(1)} %copy-done.14), channel_id=1, source_target_pairs={{0,16},{8,24},{16,0},{24,8},{1,17},{9,25},{17,1},{25,9},{2,18},{10... | collective-permute-start | bytes 208904 | tf_op jit(solution)/shard_map/ppermute | solution.py:429
  19.1 5.3 %collective-permute-start = (bf16[272,128]{1,0:T(8,128)(2,1)S(1)}, bf16[272,128]{1,0:T(8,128)(2,1)S(1)}, u32[]{:S(2)}, u32[]{:S(2)}) collective-permute-start(bf16[272,128]{1,0:T(8,128)(2,1)S(1)} %copy-done.14), channel_id=1, source_target_pairs={{0,8},{8,16},{16,24},{24,0},{1,9},{9,17},{17,25},{25,1},{2,10},{10... | collective-permute-start | bytes 208904 | tf_op jit(solution)/shard_map/ppermute | solution.py:429
  42.8 32.7 %all-to-all-start.1 = ((bf16[8,4,128,128]{3,2,1,0:T(8,128)(2,1)}), bf16[8,4,128,128]{3,2,1,0:T(8,128)(2,1)S(1)}, u32[]{:S(2)}, u32[]{:S(2)}) async-start(bf16[8,4,128,128]{3,2,1,0:T(8,128)(2,1)} %get-tuple-element.27), calls=%async_computation.1 | async-start | bytes 2097152 | tf_op jit(solution)/shard_map/all_to_all | solution.py:431
  49.7 25.8 %collective-permute-start.3 = (bf16[8,264,128]{2,1,0:T(8,128)(2,1)}, bf16[8,264,128]{2,1,0:T(8,128)(2,1)S(1)}, u32[]{:S(2)}, u32[]{:S(2)}) collective-permute-start(bf16[8,264,128]{2,1,0:T(8,128)(2,1)} %get-tuple-element.24), channel_id=1, source_target_pairs={{0,8},{8,16},{16,24},{24,0},{1,9},{9,17},{17,25},{25,1},{2,10},{10... | collective-permute-start | bytes 1622024 | tf_op jit(solution)/shard_map/ppermute | solution.py:433
  52.8 22.7 %collective-permute-start.4 = (bf16[8,264,128]{2,1,0:T(8,128)(2,1)}, bf16[8,264,128]{2,1,0:T(8,128)(2,1)S(1)}, u32[]{:S(2)}, u32[]{:S(2)}) collective-permute-start(bf16[8,264,128]{2,1,0:T(8,128)(2,1)} %get-tuple-element.25), channel_id=1, source_target_pairs={{0,16},{8,24},{16,0},{24,8},{1,17},{9,25},{17,1},{25,9},{2,18},{10... | collective-permute-start | bytes 1622024 | tf_op jit(solution)/shard_map/ppermute | solution.py:433
  55.6 26.6 %collective-permute-start.5 = (bf16[8,264,128]{2,1,0:T(8,128)(2,1)}, bf16[8,264,128]{2,1,0:T(8,128)(2,1)S(1)}, u32[]{:S(2)}, u32[]{:S(2)}) collective-permute-start(bf16[8,264,128]{2,1,0:T(8,128)(2,1)} %get-tuple-element.26), channel_id=1, source_target_pairs={{0,24},{8,0},{16,8},{24,16},{1,25},{9,1},{17,9},{25,17},{2,26},{10... | collective-permute-start | bytes 1622024 | tf_op jit(solution)/shard_map/ppermute | solution.py:433
  94.1 93.1 %all-to-all-start.2 = ((bf16[32,384,128]{2,1,0:T(8,128)(2,1)}), bf16[32,384,128]{2,1,0:T(8,128)(2,1)S(1)}, u32[]{:S(2)}, u32[]{:S(2)}) async-start(bf16[32,384,128]{2,1,0:T(8,128)(2,1)} %get-tuple-element.28), calls=%async_computation.2 | async-start | bytes 6291456 | tf_op jit(solution)/shard_map/all_to_all | solution.py:435
  102.2 6.7 %collective-permute-start.6 = (f32[8,64,768]{2,1,0:T(8,128)}, f32[8,64,768]{2,1,0:T(8,128)}, u32[]{:S(2)}, u32[]{:S(2)}) collective-permute-start(f32[8,64,768]{2,1,0:T(8,128)} %get-tuple-element.30), channel_id=1, source_target_pairs={{0,32},{32,0},{64,96},{96,64},{128,160},{160,128},{192,224},{224,1... | collective-permute-start | bytes 4718600 | tf_op jit(solution)/shard_map/ppermute | solution.py:437
  111.8 30.9 %copy-start.11 = (f32[1,64,768]{2,1,0:T(8,128)S(1)}, f32[1,64,768]{2,1,0:T(8,128)}, u32[]{:S(2)}) copy-start(f32[1,64,768]{2,1,0:T(8,128)} %param.10) | copy-start | bytes 589828
  111.8 30.9 %copy-start.12 = (f32[1,64,768]{2,1,0:T(8,128)S(1)}, f32[1,64,768]{2,1,0:T(8,128)}, u32[]{:S(2)}) copy-start(f32[1,64,768]{2,1,0:T(8,128)} %param.11) | copy-start | bytes 589828
  111.8 17.6 %collective-permute-start.7 = (bf16[128,768]{1,0:T(8,128)(2,1)}, bf16[128,768]{1,0:T(8,128)(2,1)}, u32[]{:S(2)}, u32[]{:S(2)}) collective-permute-start(bf16[128,768]{1,0:T(8,128)(2,1)} %get-tuple-element.32), channel_id=1, source_target_pairs={{0,64},{32,480},{64,128},{96,32},{128,192},{160,96},{192,256},{224... | collective-permute-start | bytes 589832 | tf_op jit(solution)/shard_map/ppermute | solution.py:441
  117.0 12.4 %collective-permute-start.8 = (bf16[128,768]{1,0:T(8,128)(2,1)}, bf16[128,768]{1,0:T(8,128)(2,1)}, u32[]{:S(2)}, u32[]{:S(2)}) collective-permute-start(bf16[128,768]{1,0:T(8,128)(2,1)} %get-tuple-element.33), channel_id=1, source_target_pairs={{0,128},{32,416},{64,192},{96,480},{128,256},{160,32},{192,320},{2... | collective-permute-start | bytes 589832 | tf_op jit(solution)/shard_map/ppermute | solution.py:441
  120.8 9.2 %collective-permute-start.9 = (bf16[128,768]{1,0:T(8,128)(2,1)}, bf16[128,768]{1,0:T(8,128)(2,1)}, u32[]{:S(2)}, u32[]{:S(2)}) collective-permute-start(bf16[128,768]{1,0:T(8,128)(2,1)} %get-tuple-element.34), channel_id=1, source_target_pairs={{0,192},{32,352},{64,256},{96,416},{128,320},{160,480},{192,384},{... | collective-permute-start | bytes 589832 | tf_op jit(solution)/shard_map/ppermute | solution.py:441
  123.5 12.0 %collective-permute-start.10 = (bf16[64,768]{1,0:T(8,128)(2,1)}, bf16[64,768]{1,0:T(8,128)(2,1)S(1)}, u32[]{:S(2)}, u32[]{:S(2)}) collective-permute-start(bf16[64,768]{1,0:T(8,128)(2,1)} %get-tuple-element.35), channel_id=1, source_target_pairs={{0,256},{32,288},{64,320},{96,352},{128,384},{160,416},{192,448},{... | collective-permute-start | bytes 294920 | tf_op jit(solution)/shard_map/ppermute | solution.py:443
  135.5 7.1 %collective-permute-start.11 = (f32[64,768]{1,0:T(8,128)S(1)}, f32[64,768]{1,0:T(8,128)S(1)}, u32[]{:S(2)}, u32[]{:S(2)}) collective-permute-start(f32[64,768]{1,0:T(8,128)S(1)} %fusion.4), channel_id=1, source_target_pairs={{0,32},{32,0},{64,96},{96,64},{128,160},{160,128},{192,224},{224,1... | collective-permute-start | bytes 589832 | tf_op jit(solution)/shard_map/ppermute | solution.py:447
  143.5 3.2 %collective-permute-start.13 = (bf16[64,768]{1,0:T(8,128)(2,1)S(1)}, bf16[64,768]{1,0:T(8,128)(2,1)S(1)}, u32[]{:S(2)}, u32[]{:S(2)}) collective-permute-start(bf16[64,768]{1,0:T(8,128)(2,1)S(1)} %get-tuple-element.36), channel_id=1, source_target_pairs={{0,32},{32,0},{64,96},{96,64},{128,160},{160,128},{192,224},{224,1... | collective-permute-start | bytes 294920 | tf_op jit(solution)/shard_map/ppermute | solution.py:455
  146.8 31.2 %copy-start.3 = (bf16[128,768]{1,0:T(8,128)(2,1)}, bf16[128,768]{1,0:T(8,128)(2,1)S(1)}, u32[]{:S(2)}) copy-start(bf16[128,768]{1,0:T(8,128)(2,1)S(1)} %pad_maximum_fusion.1.both_ref) | copy-start | bytes 589828
  146.8 26.2 %collective-permute-start.16 = (bf16[128,768]{1,0:T(8,128)(2,1)S(1)}, bf16[128,768]{1,0:T(8,128)(2,1)S(1)}, u32[]{:S(2)}, u32[]{:S(2)}) collective-permute-start(bf16[128,768]{1,0:T(8,128)(2,1)S(1)} %pad_maximum_fusion.1.both_ref), channel_id=1, source_target_pairs={{0,192},{32,352},{64,256},{96,416},{128,320},{160,480},{192,384},{... | collective-permute-start | bytes 589832 | tf_op jit(solution)/shard_map/ppermute | solution.py:459
  151.8 21.2 %collective-permute-start.15 = (bf16[128,768]{1,0:T(8,128)(2,1)S(1)}, bf16[128,768]{1,0:T(8,128)(2,1)S(1)}, u32[]{:S(2)}, u32[]{:S(2)}) collective-permute-start(bf16[128,768]{1,0:T(8,128)(2,1)S(1)} %pad_maximum_fusion.1.both_ref), channel_id=1, source_target_pairs={{0,128},{32,416},{64,192},{96,480},{128,256},{160,32},{192,320},{2... | collective-permute-start | bytes 589832 | tf_op jit(solution)/shard_map/ppermute | solution.py:459
  154.0 19.1 %collective-permute-start.14 = (bf16[128,768]{1,0:T(8,128)(2,1)S(1)}, bf16[128,768]{1,0:T(8,128)(2,1)S(1)}, u32[]{:S(2)}, u32[]{:S(2)}) collective-permute-start(bf16[128,768]{1,0:T(8,128)(2,1)S(1)} %pad_maximum_fusion.1.both_ref), channel_id=1, source_target_pairs={{0,64},{32,480},{64,128},{96,32},{128,192},{160,96},{192,256},{224... | collective-permute-start | bytes 589832 | tf_op jit(solution)/shard_map/ppermute | solution.py:459
  159.5 13.5 %collective-permute-start.12 = (bf16[64,768]{1,0:T(8,128)(2,1)S(1)}, bf16[64,768]{1,0:T(8,128)(2,1)S(1)}, u32[]{:S(2)}, u32[]{:S(2)}) collective-permute-start(bf16[64,768]{1,0:T(8,128)(2,1)S(1)} %get-tuple-element.36), channel_id=1, source_target_pairs={{0,256},{32,288},{64,320},{96,352},{128,384},{160,416},{192,448},{... | collective-permute-start | bytes 294920 | tf_op jit(solution)/shard_map/ppermute | solution.py:454
  174.7 7.9 %collective-permute-start.17 = (bf16[448,768]{1,0:T(8,128)(2,1)}, bf16[448,768]{1,0:T(8,128)(2,1)}, u32[]{:S(2)}, u32[]{:S(2)}) collective-permute-start(bf16[448,768]{1,0:T(8,128)(2,1)} %pad_maximum_fusion), channel_id=1, source_target_pairs={{0,32},{32,0},{64,96},{96,64},{128,160},{160,128},{192,224},{224,1... | collective-permute-start | bytes 2064392 | tf_op jit(solution)/shard_map/ppermute | solution.py:460
  (15 other events, 67.0 us)
where the time goes:
time: 194 us; the launch traced here: 193 us
  starting transfers between devices  90.2 us (46%)
  waiting for transfers between devices  58.9 us (30%)
  Pallas kernels  35.4 us (18%)
  local copies, waits for them, and re-layouts  3.88 us (2%)
  other arithmetic  3.7 us (2%)
    all_to_all x1, waiting for transfers between devices, body(): lax.all_to_all(across, 'z', split_axis=0, concat_axis=0, tiled=True)  16.2 us
    all_to_all x1, waiting for transfers between devices, body(): up = lax.all_to_all(up, 'z', split_axis=0, concat_axis=0, tiled=True)  14.9 us
    ppermute x3, starting transfers between devices, body(): near = [lax.ppermute(both, 'rep', along_y(i + 1)) for i in range(FAR)]  12.7 us
    ppermute x3, starting transfers between devices, body(): side = side + lax.ppermute(share, 'rep', along_y(i + 1)).astype(f32)  11.7 us
    pallas_call x1, Pallas kernels, label_blocks(): pl.pallas_call(block_kernel, grid=(pairs,), in_specs=[pl.BlockSpec(memory...  11 us
    all_to_all x1, starting transfers between devices, body(): up = lax.all_to_all(up, 'z', split_axis=0, concat_axis=0, tiled=True)  10.2 us
    ppermute x3, starting transfers between devices, body(): lax.ppermute(across, 'x', along_x(t))  9.64 us
    ppermute x3, starting transfers between devices, body(): up = [up[0]] + [lax.ppermute(up[t], 'x', along_x(t)) for t in range(1, N_X)]  9.62 us
  transfers between devices with their start and end apart: 21, of which 10 were waited for; matrix products, arithmetic and copies ran while one was open for 2% of the time, Pallas kernels for 9%

commit v1 on v0

--- a/solution.py
+++ b/solution.py
@@ -23,6 +23,7 @@
 SLOTS = BLK_DEV * CAP
 CHUNK = COLS * SLOTS
 SUB = 64
+MIB = 1 << 20
 FAR = N_Y // 2 - 1
 
 beta_first = 0.9
@@ -225,13 +226,12 @@
                 give_ref[at] = grad[i * SUB : (i + 1) * SUB]
 
     for c in range(COLS):
-        at = pl.ds(pl.multiple_of(c * SLOTS + pair * 2 * CAP, 2 * CAP), 2 * CAP)
         cols = slice(c * LANES, (c + 1) * LANES)
         both = jnp.stack([p[:, cols].reshape(N_LAB, CAP, LANES) for p in parts], axis=1)
         both = both.reshape(N_LAB, 2 * CAP, LANES).astype(bf16)
         for t in range(N_X):
             source_x = lax.rem(x - t + N_X, N_X)
-            back_ref[pl.ds(source_x * N_Z, N_Z), at, :] = both[t * N_Z : (t + 1) * N_Z]
+            back_ref[pl.ds(source_x * N_Z, N_Z), c, 0] = both[t * N_Z : (t + 1) * N_Z]
 
 
 def label_blocks(where, up, across, label_weight):
@@ -248,12 +248,12 @@
             pl.BlockSpec((2 * BLOCK, D), lambda p: (p, 0)),
         ],
         out_specs=[
-            pl.BlockSpec((N_LAB, CHUNK, LANES), lambda p: (0, 0, 0)),
+            pl.BlockSpec((N_LAB, COLS, 1, 2 * CAP, LANES), lambda p: (0, 0, p, 0, 0)),
             pl.BlockSpec((N_Y, SUB, D), lambda p: (0, 0, 0)),
             pl.BlockSpec((N_Y, SUB, D), lambda p: (0, 0, 0)),
         ],
         out_shape=(
-            jax.ShapeDtypeStruct((N_LAB, CHUNK, LANES), bf16),
+            jax.ShapeDtypeStruct((N_LAB, COLS, pairs, 2 * CAP, LANES), bf16),
             jax.ShapeDtypeStruct((BLK_DEV, SUB, D), f32),
             jax.ShapeDtypeStruct((BLK_DEV, SUB, D), f32),
         ),
@@ -302,6 +302,7 @@
         out_shape=jax.ShapeDtypeStruct((LANES, D), f32),
         cost_estimate=pl.CostEstimate(flops=400_000_000, bytes_accessed=4_000_000, transcendentals=0),
         name="sum_parts",
+        compiler_params=pltpu.CompilerParams(vmem_limit_bytes=16 * MIB),
     )(pick, back)
 
 
@@ -387,6 +388,7 @@
         out_shape=out_shape,
         cost_estimate=cost,
         name="near_weight",
+        compiler_params=pltpu.CompilerParams(vmem_limit_bytes=10 * MIB),
     )(where, label_weight, both, *near)
     return pl.pallas_call(
         far_kernel,
@@ -405,6 +407,7 @@
         input_output_aliases={4: 0},
         cost_estimate=cost,
         name="far_weight",
+        compiler_params=pltpu.CompilerParams(vmem_limit_bytes=10 * MIB),
     )(where, label_weight, opposite, other, begun)
 
 
@@ -432,8 +435,8 @@
     up = select_up(where, up)
     up = [up[0]] + [lax.ppermute(up[t], "x", along_x(t)) for t in range(1, N_X)]
     back, keep, give = label_blocks(where, up, across, label_weight)
+    back = back.reshape(N_LAB, CHUNK, LANES)
     returned = lax.all_to_all(back, ("x", "z"), split_axis=0, concat_axis=0, tiled=True)
-
     got = lax.ppermute(give, "rep", OTHER_CORE)
     *sides, opposite, grad = split_by_y(keep, got)
     side = jnp.zeros((BLOCK, D), f32)

time: 194 us -> 185 us (0.954)
  Pallas kernels: 35.4 us -> 28.1 us
    pallas_call x1, Pallas kernels: 4.55 us -> 2.35 us  [fresh_weight(): pl.pallas_call(near_kernel, grid_spec=pltpu.PrefetchScalarGridSpec(num_sc...]
    pallas_call x1, Pallas kernels: 4.55 us -> 2.37 us  [fresh_weight(): pl.pallas_call(far_kernel, grid_spec=pltpu.PrefetchScalarGridSpec(num_sca...]
    pallas_call x1, Pallas kernels: 4.24 us -> 2.13 us  [sum_parts(): pl.pallas_call(sum_kernel, grid=(steps,), in_specs=[pl.BlockSpec((groups...]
    unnamed x36 -> x30, local copies, waits for them, and re-layouts: 3.88 us -> 2.56 us
  transfers between devices with their start and end apart: 21 -> 21, of which waited for: 10 -> 10; matrix products, arithmetic and copies ran while one was open for 2% -> 2% of each run, Pallas kernels for 9% -> 7%
where the time goes in v1:
time: 185 us; the launch traced here: 184 us
  starting transfers between devices  90.4 us (49%)
  waiting for transfers between devices  58.8 us (32%)
  Pallas kernels  28.1 us (15%)
  other arithmetic  2.88 us (2%)
  local copies, waits for them, and re-layouts  2.56 us (1%)
    all_to_all x1, waiting for transfers between devices, body(): lax.all_to_all(across, 'z', split_axis=0, concat_axis=0, tiled=True)  16.2 us
    all_to_all x1, waiting for transfers between devices, body(): up = lax.all_to_all(up, 'z', split_axis=0, concat_axis=0, tiled=True)  14.9 us
    ppermute x3, starting transfers between devices, body(): near = [lax.ppermute(both, 'rep', along_y(i + 1)) for i in range(FAR)]  12.7 us
    ppermute x3, starting transfers between devices, body(): side = side + lax.ppermute(share, 'rep', along_y(i + 1)).astype(f32)  11.7 us
    pallas_call x1, Pallas kernels, label_blocks(): pl.pallas_call(block_kernel, grid=(pairs,), in_specs=[pl.BlockSpec(memory...  10.2 us
    all_to_all x1, starting transfers between devices, body(): up = lax.all_to_all(up, 'z', split_axis=0, concat_axis=0, tiled=True)  10.2 us
    ppermute x3, starting transfers between devices, body(): lax.ppermute(across, 'x', along_x(t))  9.64 us
    ppermute x3, starting transfers between devices, body(): up = [up[0]] + [lax.ppermute(up[t], 'x', along_x(t)) for t in range(1, N_X)]  9.62 us
  transfers between devices with their start and end apart: 21, of which 10 were waited for; matrix products, arithmetic and copies ran while one was open for 2% of the time, Pallas kernels for 7%

profile of v1, /device:TPU:3, one launch (start us, length us, event | category | flops | bytes accessed | tf_op | source)
XLA Modules:
  0.0 183.7 jit_solution(11251597993104272213)
XLA Ops:
  2.7 10.2 %all-to-all-start = ((bf16[8,528,128]{2,1,0:T(8,128)(2,1)}), bf16[8,528,128]{2,1,0:T(8,128)(2,1)S(1)}, u32[]{:S(2)}, u32[]{:S(2)}) async-start(bf16[8,528,128]{2,1,0:T(8,128)(2,1)} %get-tuple-element.22), calls=%async_computation | async-start | bytes 2162688 | tf_op jit(solution)/shard_map/all_to_all | solution.py:431
  15.1 4.0 %collective-permute-start.1 = (bf16[272,128]{1,0:T(8,128)(2,1)S(1)}, bf16[272,128]{1,0:T(8,128)(2,1)S(1)}, u32[]{:S(2)}, u32[]{:S(2)}) collective-permute-start(bf16[272,128]{1,0:T(8,128)(2,1)S(1)} %copy-done.11), channel_id=1, source_target_pairs={{0,16},{8,24},{16,0},{24,8},{1,17},{9,25},{17,1},{25,9},{2,18},{10... | collective-permute-start | bytes 208904 | tf_op jit(solution)/shard_map/ppermute | solution.py:432
  19.1 3.4 %collective-permute-start = (bf16[272,128]{1,0:T(8,128)(2,1)S(1)}, bf16[272,128]{1,0:T(8,128)(2,1)S(1)}, u32[]{:S(2)}, u32[]{:S(2)}) collective-permute-start(bf16[272,128]{1,0:T(8,128)(2,1)S(1)} %copy-done.11), channel_id=1, source_target_pairs={{0,8},{8,16},{16,24},{24,0},{1,9},{9,17},{17,25},{25,1},{2,10},{10... | collective-permute-start | bytes 208904 | tf_op jit(solution)/shard_map/ppermute | solution.py:432
  27.9 14.9 %all-to-all-done.arrived_ref = bf16[8,528,128]{2,1,0:T(8,128)(2,1)S(1)} async-done(((bf16[8,528,128]{2,1,0:T(8,128)(2,1)}), bf16[8,528,128]{2,1,0:T(8,128)(2,1)S(1)}, u32[]{:S(2)}, u32[]{:S(2)}) %all-to-all-start) | async-done | bytes 1081376 | tf_op jit(solution)/shard_map/all_to_all | solution.py:431
  42.8 3.6 %all-to-all-start.1 = ((bf16[8,4,128,128]{3,2,1,0:T(8,128)(2,1)}), bf16[8,4,128,128]{3,2,1,0:T(8,128)(2,1)S(1)}, u32[]{:S(2)}, u32[]{:S(2)}) async-start(bf16[8,4,128,128]{3,2,1,0:T(8,128)(2,1)} %get-tuple-element.27), calls=%async_computation.1 | async-start | bytes 2097152 | tf_op jit(solution)/shard_map/all_to_all | solution.py:434
  46.4 3.3 %select_up.1 = (bf16[8,264,128]{2,1,0:T(8,128)(2,1)}, bf16[8,264,128]{2,1,0:T(8,128)(2,1)}, bf16[8,264,128]{2,1,0:T(8,128)(2,1)}, bf16[8,264,128]{2,1,0:T(8,128)(2,1)}) custom-call(s32[4]{0:T(128)} %pad_add_fusion.where_ref, bf16[8,528,128]{2,1,0:T(8,128)(2,1)} %copy-done.4), custom_call_target="tpu_custom_call" | custom-call | flops 300000000 | bytes 3000000 | tf_op jit(solution)/shard_map/select_up/pallas_call | solution.py:159
  49.7 3.1 %collective-permute-start.3 = (bf16[8,264,128]{2,1,0:T(8,128)(2,1)}, bf16[8,264,128]{2,1,0:T(8,128)(2,1)S(1)}, u32[]{:S(2)}, u32[]{:S(2)}) collective-permute-start(bf16[8,264,128]{2,1,0:T(8,128)(2,1)} %get-tuple-element.24), channel_id=1, source_target_pairs={{0,8},{8,16},{16,24},{24,0},{1,9},{9,17},{17,25},{25,1},{2,10},{10... | collective-permute-start | bytes 1622024 | tf_op jit(solution)/shard_map/ppermute | solution.py:436
  55.6 3.8 %collective-permute-start.5 = (bf16[8,264,128]{2,1,0:T(8,128)(2,1)}, bf16[8,264,128]{2,1,0:T(8,128)(2,1)S(1)}, u32[]{:S(2)}, u32[]{:S(2)}) collective-permute-start(bf16[8,264,128]{2,1,0:T(8,128)(2,1)} %get-tuple-element.26), channel_id=1, source_target_pairs={{0,24},{8,0},{16,8},{24,16},{1,25},{9,1},{17,9},{25,17},{2,26},{10... | collective-permute-start | bytes 1622024 | tf_op jit(solution)/shard_map/ppermute | solution.py:436
  59.3 16.2 %all-to-all-done.1.b_ref = bf16[8,4,128,128]{3,2,1,0:T(8,128)(2,1)S(1)} async-done(((bf16[8,4,128,128]{3,2,1,0:T(8,128)(2,1)}), bf16[8,4,128,128]{3,2,1,0:T(8,128)(2,1)S(1)}, u32[]{:S(2)}, u32[]{:S(2)}) %all-to-all-start.1) | async-done | bytes 1048608 | tf_op jit(solution)/shard_map/all_to_all | solution.py:434
  75.5 6.7 %collective-permute-done.5.a3_ref = bf16[8,264,128]{2,1,0:T(8,128)(2,1)S(1)} collective-permute-done((bf16[8,264,128]{2,1,0:T(8,128)(2,1)}, bf16[8,264,128]{2,1,0:T(8,128)(2,1)S(1)}, u32[]{:S(2)}, u32[]{:S(2)}) %collective-permute-start.5) | collective-permute-done | bytes 540704 | tf_op jit(solution)/shard_map/ppermute | solution.py:436
  83.1 10.2 %label_blocks.1 = (bf16[32,6,4,16,128]{4,3,2,1,0:T(8,128)(2,1)}, f32[8,64,768]{2,1,0:T(8,128)}, f32[8,64,768]{2,1,0:T(8,128)}) custom-call(s32[4]{0:T(128)} %pad_add_fusion.where_ref, bf16[8,264,128]{2,1,0:T(8,128)(2,1)} %get-tuple-element.23.a0_ref, bf16[8,264,128]{2,1,0:T(8,128)(2,1)} %copy-done.5, bf16[8,264,128]{2,1,0:T(8,128)(2,1)} %copy-done.6, ...), custom_call_target="tpu_custom_call" | custom-call | flops 1210000000 | bytes 11000000 | tf_op jit(solution)/shard_map/label_blocks/pallas_call | solution.py:239
  93.3 8.1 %all-to-all-start.2 = ((bf16[32,384,128]{2,1,0:T(8,128)(2,1)}), bf16[32,384,128]{2,1,0:T(8,128)(2,1)S(1)}, u32[]{:S(2)}, u32[]{:S(2)}) async-start(bf16[32,384,128]{2,1,0:T(8,128)(2,1)} %bitcast.17), calls=%async_computation.2 | async-start | bytes 6291456 | tf_op jit(solution)/shard_map/all_to_all | solution.py:439
  101.5 3.3 %collective-permute-start.6 = (f32[8,64,768]{2,1,0:T(8,128)}, f32[8,64,768]{2,1,0:T(8,128)}, u32[]{:S(2)}, u32[]{:S(2)}) collective-permute-start(f32[8,64,768]{2,1,0:T(8,128)} %get-tuple-element.30), channel_id=1, source_target_pairs={{0,32},{32,0},{64,96},{96,64},{128,160},{160,128},{192,224},{224,1... | collective-permute-start | bytes 4718600 | tf_op jit(solution)/shard_map/ppermute | solution.py:440
  104.8 3.4 %collective-permute-done.6.got_ref = f32[8,64,768]{2,1,0:T(8,128)} collective-permute-done((f32[8,64,768]{2,1,0:T(8,128)}, f32[8,64,768]{2,1,0:T(8,128)}, u32[]{:S(2)}, u32[]{:S(2)}) %collective-permute-start.6) | collective-permute-done | bytes 1572896 | tf_op jit(solution)/shard_map/ppermute | solution.py:440
  111.0 5.2 %collective-permute-start.7 = (bf16[128,768]{1,0:T(8,128)(2,1)}, bf16[128,768]{1,0:T(8,128)(2,1)}, u32[]{:S(2)}, u32[]{:S(2)}) collective-permute-start(bf16[128,768]{1,0:T(8,128)(2,1)} %get-tuple-element.32), channel_id=1, source_target_pairs={{0,64},{32,480},{64,128},{96,32},{128,192},{160,96},{192,256},{224... | collective-permute-start | bytes 589832 | tf_op jit(solution)/shard_map/ppermute | solution.py:444
  116.2 3.8 %collective-permute-start.8 = (bf16[128,768]{1,0:T(8,128)(2,1)}, bf16[128,768]{1,0:T(8,128)(2,1)}, u32[]{:S(2)}, u32[]{:S(2)}) collective-permute-start(bf16[128,768]{1,0:T(8,128)(2,1)} %get-tuple-element.33), channel_id=1, source_target_pairs={{0,128},{32,416},{64,192},{96,480},{128,256},{160,32},{192,320},{2... | collective-permute-start | bytes 589832 | tf_op jit(solution)/shard_map/ppermute | solution.py:444
  122.7 5.8 %collective-permute-start.10 = (bf16[64,768]{1,0:T(8,128)(2,1)}, bf16[64,768]{1,0:T(8,128)(2,1)S(1)}, u32[]{:S(2)}, u32[]{:S(2)}) collective-permute-start(bf16[64,768]{1,0:T(8,128)(2,1)} %get-tuple-element.35), channel_id=1, source_target_pairs={{0,256},{32,288},{64,320},{96,352},{128,384},{160,416},{192,448},{... | collective-permute-start | bytes 294920 | tf_op jit(solution)/shard_map/ppermute | solution.py:446
  130.3 4.3 %collective-permute-done.10 = bf16[64,768]{1,0:T(8,128)(2,1)S(1)} collective-permute-done((bf16[64,768]{1,0:T(8,128)(2,1)}, bf16[64,768]{1,0:T(8,128)(2,1)S(1)}, u32[]{:S(2)}, u32[]{:S(2)}) %collective-permute-start.10) | collective-permute-done | bytes 98336 | tf_op jit(solution)/shard_map/ppermute | solution.py:446
  134.7 6.0 %collective-permute-start.11 = (f32[64,768]{1,0:T(8,128)S(1)}, f32[64,768]{1,0:T(8,128)S(1)}, u32[]{:S(2)}, u32[]{:S(2)}) collective-permute-start(f32[64,768]{1,0:T(8,128)S(1)} %fusion.4), channel_id=1, source_target_pairs={{0,32},{32,0},{64,96},{96,64},{128,160},{160,128},{192,224},{224,1... | collective-permute-start | bytes 589832 | tf_op jit(solution)/shard_map/ppermute | solution.py:450
  146.1 5.0 %collective-permute-start.16 = (bf16[128,768]{1,0:T(8,128)(2,1)S(1)}, bf16[128,768]{1,0:T(8,128)(2,1)S(1)}, u32[]{:S(2)}, u32[]{:S(2)}) collective-permute-start(bf16[128,768]{1,0:T(8,128)(2,1)S(1)} %pad_maximum_fusion.1.both_ref), channel_id=1, source_target_pairs={{0,192},{32,352},{64,256},{96,416},{128,320},{160,480},{192,384},{... | collective-permute-start | bytes 589832 | tf_op jit(solution)/shard_map/ppermute | solution.py:462
  153.3 5.5 %collective-permute-start.14 = (bf16[128,768]{1,0:T(8,128)(2,1)S(1)}, bf16[128,768]{1,0:T(8,128)(2,1)S(1)}, u32[]{:S(2)}, u32[]{:S(2)}) collective-permute-start(bf16[128,768]{1,0:T(8,128)(2,1)S(1)} %pad_maximum_fusion.1.both_ref), channel_id=1, source_target_pairs={{0,64},{32,480},{64,128},{96,32},{128,192},{160,96},{192,256},{224... | collective-permute-start | bytes 589832 | tf_op jit(solution)/shard_map/ppermute | solution.py:462
  158.8 3.9 %collective-permute-start.12 = (bf16[64,768]{1,0:T(8,128)(2,1)S(1)}, bf16[64,768]{1,0:T(8,128)(2,1)S(1)}, u32[]{:S(2)}, u32[]{:S(2)}) collective-permute-start(bf16[64,768]{1,0:T(8,128)(2,1)S(1)} %get-tuple-element.36), channel_id=1, source_target_pairs={{0,256},{32,288},{64,320},{96,352},{128,384},{160,416},{192,448},{... | collective-permute-start | bytes 294920 | tf_op jit(solution)/shard_map/ppermute | solution.py:457
  162.8 9.6 %collective-permute-done.12.mine_ref = bf16[64,768]{1,0:T(8,128)(2,1)S(1)} collective-permute-done((bf16[64,768]{1,0:T(8,128)(2,1)S(1)}, bf16[64,768]{1,0:T(8,128)(2,1)S(1)}, u32[]{:S(2)}, u32[]{:S(2)}) %collective-permute-start.12) | collective-permute-done | bytes 98336 | tf_op jit(solution)/shard_map/ppermute | solution.py:457
  172.4 3.3 %collective-permute-start.17 = (bf16[448,768]{1,0:T(8,128)(2,1)S(1)}, bf16[448,768]{1,0:T(8,128)(2,1)S(1)}, u32[]{:S(2)}, u32[]{:S(2)}) collective-permute-start(bf16[448,768]{1,0:T(8,128)(2,1)S(1)} %pad_maximum_fusion), channel_id=1, source_target_pairs={{0,32},{32,0},{64,96},{96,64},{128,160},{160,128},{192,224},{224,1... | collective-permute-start | bytes 2064392 | tf_op jit(solution)/shard_map/ppermute | solution.py:463
  (63 shorter events, 36.0 us)
Async XLA Ops:
  2.7 40.1 %all-to-all-start = ((bf16[8,528,128]{2,1,0:T(8,128)(2,1)}), bf16[8,528,128]{2,1,0:T(8,128)(2,1)S(1)}, u32[]{:S(2)}, u32[]{:S(2)}) async-start(bf16[8,528,128]{2,1,0:T(8,128)(2,1)} %get-tuple-element.22), calls=%async_computation | async-start | bytes 2162688 | tf_op jit(solution)/shard_map/all_to_all | solution.py:431
  12.9 10.4 %collective-permute-start.2 = (bf16[272,128]{1,0:T(8,128)(2,1)S(1)}, bf16[272,128]{1,0:T(8,128)(2,1)S(1)}, u32[]{:S(2)}, u32[]{:S(2)}) collective-permute-start(bf16[272,128]{1,0:T(8,128)(2,1)S(1)} %copy-done.11), channel_id=1, source_target_pairs={{0,24},{8,0},{16,8},{24,16},{1,25},{9,1},{17,9},{25,17},{2,26},{10... | collective-permute-start | bytes 208904 | tf_op jit(solution)/shard_map/ppermute | solution.py:432
  15.1 8.2 %collective-permute-start.1 = (bf16[272,128]{1,0:T(8,128)(2,1)S(1)}, bf16[272,128]{1,0:T(8,128)(2,1)S(1)}, u32[]{:S(2)}, u32[]{:S(2)}) collective-permute-start(bf16[272,128]{1,0:T(8,128)(2,1)S(1)} %copy-done.11), channel_id=1, source_target_pairs={{0,16},{8,24},{16,0},{24,8},{1,17},{9,25},{17,1},{25,9},{2,18},{10... | collective-permute-start | bytes 208904 | tf_op jit(solution)/shard_map/ppermute | solution.py:432
  19.1 5.3 %collective-permute-start = (bf16[272,128]{1,0:T(8,128)(2,1)S(1)}, bf16[272,128]{1,0:T(8,128)(2,1)S(1)}, u32[]{:S(2)}, u32[]{:S(2)}) collective-permute-start(bf16[272,128]{1,0:T(8,128)(2,1)S(1)} %copy-done.11), channel_id=1, source_target_pairs={{0,8},{8,16},{16,24},{24,0},{1,9},{9,17},{17,25},{25,1},{2,10},{10... | collective-permute-start | bytes 208904 | tf_op jit(solution)/shard_map/ppermute | solution.py:432
  42.8 32.7 %all-to-all-start.1 = ((bf16[8,4,128,128]{3,2,1,0:T(8,128)(2,1)}), bf16[8,4,128,128]{3,2,1,0:T(8,128)(2,1)S(1)}, u32[]{:S(2)}, u32[]{:S(2)}) async-start(bf16[8,4,128,128]{3,2,1,0:T(8,128)(2,1)} %get-tuple-element.27), calls=%async_computation.1 | async-start | bytes 2097152 | tf_op jit(solution)/shard_map/all_to_all | solution.py:434
  49.7 25.8 %collective-permute-start.3 = (bf16[8,264,128]{2,1,0:T(8,128)(2,1)}, bf16[8,264,128]{2,1,0:T(8,128)(2,1)S(1)}, u32[]{:S(2)}, u32[]{:S(2)}) collective-permute-start(bf16[8,264,128]{2,1,0:T(8,128)(2,1)} %get-tuple-element.24), channel_id=1, source_target_pairs={{0,8},{8,16},{16,24},{24,0},{1,9},{9,17},{17,25},{25,1},{2,10},{10... | collective-permute-start | bytes 1622024 | tf_op jit(solution)/shard_map/ppermute | solution.py:436
  52.8 22.7 %collective-permute-start.4 = (bf16[8,264,128]{2,1,0:T(8,128)(2,1)}, bf16[8,264,128]{2,1,0:T(8,128)(2,1)S(1)}, u32[]{:S(2)}, u32[]{:S(2)}) collective-permute-start(bf16[8,264,128]{2,1,0:T(8,128)(2,1)} %get-tuple-element.25), channel_id=1, source_target_pairs={{0,16},{8,24},{16,0},{24,8},{1,17},{9,25},{17,1},{25,9},{2,18},{10... | collective-permute-start | bytes 1622024 | tf_op jit(solution)/shard_map/ppermute | solution.py:436
  55.6 26.6 %collective-permute-start.5 = (bf16[8,264,128]{2,1,0:T(8,128)(2,1)}, bf16[8,264,128]{2,1,0:T(8,128)(2,1)S(1)}, u32[]{:S(2)}, u32[]{:S(2)}) collective-permute-start(bf16[8,264,128]{2,1,0:T(8,128)(2,1)} %get-tuple-element.26), channel_id=1, source_target_pairs={{0,24},{8,0},{16,8},{24,16},{1,25},{9,1},{17,9},{25,17},{2,26},{10... | collective-permute-start | bytes 1622024 | tf_op jit(solution)/shard_map/ppermute | solution.py:436
  93.3 87.2 %all-to-all-start.2 = ((bf16[32,384,128]{2,1,0:T(8,128)(2,1)}), bf16[32,384,128]{2,1,0:T(8,128)(2,1)S(1)}, u32[]{:S(2)}, u32[]{:S(2)}) async-start(bf16[32,384,128]{2,1,0:T(8,128)(2,1)} %bitcast.17), calls=%async_computation.2 | async-start | bytes 6291456 | tf_op jit(solution)/shard_map/all_to_all | solution.py:439
  101.5 6.7 %collective-permute-start.6 = (f32[8,64,768]{2,1,0:T(8,128)}, f32[8,64,768]{2,1,0:T(8,128)}, u32[]{:S(2)}, u32[]{:S(2)}) collective-permute-start(f32[8,64,768]{2,1,0:T(8,128)} %get-tuple-element.30), channel_id=1, source_target_pairs={{0,32},{32,0},{64,96},{96,64},{128,160},{160,128},{192,224},{224,1... | collective-permute-start | bytes 4718600 | tf_op jit(solution)/shard_map/ppermute | solution.py:440
  111.0 30.9 %copy-start.9 = (f32[1,64,768]{2,1,0:T(8,128)S(1)}, f32[1,64,768]{2,1,0:T(8,128)}, u32[]{:S(2)}) copy-start(f32[1,64,768]{2,1,0:T(8,128)} %param.11) | copy-start | bytes 589828
  111.0 17.6 %collective-permute-start.7 = (bf16[128,768]{1,0:T(8,128)(2,1)}, bf16[128,768]{1,0:T(8,128)(2,1)}, u32[]{:S(2)}, u32[]{:S(2)}) collective-permute-start(bf16[128,768]{1,0:T(8,128)(2,1)} %get-tuple-element.32), channel_id=1, source_target_pairs={{0,64},{32,480},{64,128},{96,32},{128,192},{160,96},{192,256},{224... | collective-permute-start | bytes 589832 | tf_op jit(solution)/shard_map/ppermute | solution.py:444
  116.2 12.4 %collective-permute-start.8 = (bf16[128,768]{1,0:T(8,128)(2,1)}, bf16[128,768]{1,0:T(8,128)(2,1)}, u32[]{:S(2)}, u32[]{:S(2)}) collective-permute-start(bf16[128,768]{1,0:T(8,128)(2,1)} %get-tuple-element.33), channel_id=1, source_target_pairs={{0,128},{32,416},{64,192},{96,480},{128,256},{160,32},{192,320},{2... | collective-permute-start | bytes 589832 | tf_op jit(solution)/shard_map/ppermute | solution.py:444
  120.0 9.2 %collective-permute-start.9 = (bf16[128,768]{1,0:T(8,128)(2,1)}, bf16[128,768]{1,0:T(8,128)(2,1)}, u32[]{:S(2)}, u32[]{:S(2)}) collective-permute-start(bf16[128,768]{1,0:T(8,128)(2,1)} %get-tuple-element.34), channel_id=1, source_target_pairs={{0,192},{32,352},{64,256},{96,416},{128,320},{160,480},{192,384},{... | collective-permute-start | bytes 589832 | tf_op jit(solution)/shard_map/ppermute | solution.py:444
  122.7 11.9 %collective-permute-start.10 = (bf16[64,768]{1,0:T(8,128)(2,1)}, bf16[64,768]{1,0:T(8,128)(2,1)S(1)}, u32[]{:S(2)}, u32[]{:S(2)}) collective-permute-start(bf16[64,768]{1,0:T(8,128)(2,1)} %get-tuple-element.35), channel_id=1, source_target_pairs={{0,256},{32,288},{64,320},{96,352},{128,384},{160,416},{192,448},{... | collective-permute-start | bytes 294920 | tf_op jit(solution)/shard_map/ppermute | solution.py:446
  134.7 7.1 %collective-permute-start.11 = (f32[64,768]{1,0:T(8,128)S(1)}, f32[64,768]{1,0:T(8,128)S(1)}, u32[]{:S(2)}, u32[]{:S(2)}) collective-permute-start(f32[64,768]{1,0:T(8,128)S(1)} %fusion.4), channel_id=1, source_target_pairs={{0,32},{32,0},{64,96},{96,64},{128,160},{160,128},{192,224},{224,1... | collective-permute-start | bytes 589832 | tf_op jit(solution)/shard_map/ppermute | solution.py:450
  142.7 33.0 %copy-start = (bf16[1024,768]{1,0:T(8,128)(2,1)S(1)}, bf16[1024,768]{1,0:T(8,128)(2,1)}, u32[]{:S(2)}) copy-start(bf16[1024,768]{1,0:T(8,128)(2,1)} %tile_ref.3) | copy-start | bytes 4718596
  142.7 33.0 %copy-start.2 = (s32[4]{0:T(128)S(1)}, s32[4]{0:T(128)}, u32[]{:S(2)}) copy-start(s32[4]{0:T(128)} %pad_add_fusion.where_ref) | copy-start | bytes 52
  142.7 3.3 %collective-permute-start.13 = (bf16[64,768]{1,0:T(8,128)(2,1)S(1)}, bf16[64,768]{1,0:T(8,128)(2,1)S(1)}, u32[]{:S(2)}, u32[]{:S(2)}) collective-permute-start(bf16[64,768]{1,0:T(8,128)(2,1)S(1)} %get-tuple-element.36), channel_id=1, source_target_pairs={{0,32},{32,0},{64,96},{96,64},{128,160},{160,128},{192,224},{224,1... | collective-permute-start | bytes 294920 | tf_op jit(solution)/shard_map/ppermute | solution.py:458
  146.1 26.2 %collective-permute-start.16 = (bf16[128,768]{1,0:T(8,128)(2,1)S(1)}, bf16[128,768]{1,0:T(8,128)(2,1)S(1)}, u32[]{:S(2)}, u32[]{:S(2)}) collective-permute-start(bf16[128,768]{1,0:T(8,128)(2,1)S(1)} %pad_maximum_fusion.1.both_ref), channel_id=1, source_target_pairs={{0,192},{32,352},{64,256},{96,416},{128,320},{160,480},{192,384},{... | collective-permute-start | bytes 589832 | tf_op jit(solution)/shard_map/ppermute | solution.py:462
  151.1 21.2 %collective-permute-start.15 = (bf16[128,768]{1,0:T(8,128)(2,1)S(1)}, bf16[128,768]{1,0:T(8,128)(2,1)S(1)}, u32[]{:S(2)}, u32[]{:S(2)}) collective-permute-start(bf16[128,768]{1,0:T(8,128)(2,1)S(1)} %pad_maximum_fusion.1.both_ref), channel_id=1, source_target_pairs={{0,128},{32,416},{64,192},{96,480},{128,256},{160,32},{192,320},{2... | collective-permute-start | bytes 589832 | tf_op jit(solution)/shard_map/ppermute | solution.py:462
  153.3 19.0 %collective-permute-start.14 = (bf16[128,768]{1,0:T(8,128)(2,1)S(1)}, bf16[128,768]{1,0:T(8,128)(2,1)S(1)}, u32[]{:S(2)}, u32[]{:S(2)}) collective-permute-start(bf16[128,768]{1,0:T(8,128)(2,1)S(1)} %pad_maximum_fusion.1.both_ref), channel_id=1, source_target_pairs={{0,64},{32,480},{64,128},{96,32},{128,192},{160,96},{192,256},{224... | collective-permute-start | bytes 589832 | tf_op jit(solution)/shard_map/ppermute | solution.py:462
  158.8 13.5 %collective-permute-start.12 = (bf16[64,768]{1,0:T(8,128)(2,1)S(1)}, bf16[64,768]{1,0:T(8,128)(2,1)S(1)}, u32[]{:S(2)}, u32[]{:S(2)}) collective-permute-start(bf16[64,768]{1,0:T(8,128)(2,1)S(1)} %get-tuple-element.36), channel_id=1, source_target_pairs={{0,256},{32,288},{64,320},{96,352},{128,384},{160,416},{192,448},{... | collective-permute-start | bytes 294920 | tf_op jit(solution)/shard_map/ppermute | solution.py:457
  172.4 5.7 %collective-permute-start.17 = (bf16[448,768]{1,0:T(8,128)(2,1)S(1)}, bf16[448,768]{1,0:T(8,128)(2,1)S(1)}, u32[]{:S(2)}, u32[]{:S(2)}) collective-permute-start(bf16[448,768]{1,0:T(8,128)(2,1)S(1)} %pad_maximum_fusion), channel_id=1, source_target_pairs={{0,32},{32,0},{64,96},{96,64},{128,160},{160,128},{192,224},{224,1... | collective-permute-start | bytes 2064392 | tf_op jit(solution)/shard_map/ppermute | solution.py:463
  (12 other events, 88.7 us)

commit v2 on v1

--- a/solution.py
+++ b/solution.py
@@ -265,6 +265,7 @@
             flops=1_210_000_000, bytes_accessed=11_000_000, transcendentals=300_000
         ),
         name="label_blocks",
+        compiler_params=pltpu.CompilerParams(vmem_limit_bytes=50 * MIB),
     )(where, *up, across, label_weight)
 
 
@@ -302,7 +303,7 @@
         out_shape=jax.ShapeDtypeStruct((LANES, D), f32),
         cost_estimate=pl.CostEstimate(flops=400_000_000, bytes_accessed=4_000_000, transcendentals=0),
         name="sum_parts",
-        compiler_params=pltpu.CompilerParams(vmem_limit_bytes=16 * MIB),
+        compiler_params=pltpu.CompilerParams(vmem_limit_bytes=57 * MIB),
     )(pick, back)
 
 
@@ -431,9 +432,11 @@
     up = lax.all_to_all(up, "z", split_axis=0, concat_axis=0, tiled=True)
     sources = [across] + [lax.ppermute(across, "x", along_x(t)) for t in range(1, N_X)]
     across, pick = select_across(where, short_t, pos_t, sources)
+    up = select_up(where, up)
+    opposite = lax.ppermute(up[2], "x", along_x(2))
     across = lax.all_to_all(across, "z", split_axis=0, concat_axis=0, tiled=True)
-    up = select_up(where, up)
-    up = [up[0]] + [lax.ppermute(up[t], "x", along_x(t)) for t in range(1, N_X)]
+    beside = [lax.ppermute(up[t], "x", along_x(t)) for t in (1, 3)]
+    up = [up[0], beside[0], opposite, beside[1]]
     back, keep, give = label_blocks(where, up, across, label_weight)
     back = back.reshape(N_LAB, CHUNK, LANES)
     returned = lax.all_to_all(back, ("x", "z"), split_axis=0, concat_axis=0, tiled=True)

time: 185 us -> 186 us (level)
  the two profiles are of different devices: /device:TPU:3 before, /device:TPU:1 now
where the time goes in v2:
time: 186 us; the launch traced here: 185 us
  starting transfers between devices  92.5 us (50%)
  waiting for transfers between devices  57.3 us (31%)
  Pallas kernels  29.2 us (16%)
  local copies, waits for them, and re-layouts  2.89 us (2%)
    all_to_all x1, waiting for transfers between devices, body(): lax.all_to_all(across, 'z', split_axis=0, concat_axis=0, tiled=True)  15.2 us
    all_to_all x1, waiting for transfers between devices, body(): up = lax.all_to_all(up, 'z', split_axis=0, concat_axis=0, tiled=True)  12.7 us
    ppermute x3, starting transfers between devices, body(): near = [lax.ppermute(both, 'rep', along_y(i + 1)) for i in range(FAR)]  12.7 us
    ppermute x3, starting transfers between devices, body(): side = side + lax.ppermute(share, 'rep', along_y(i + 1)).astype(f32)  11.7 us
    all_to_all x1, starting transfers between devices, body(): up = lax.all_to_all(up, 'z', split_axis=0, concat_axis=0, tiled=True)  11 us
    all_to_all x1, starting transfers between devices, body(): lax.all_to_all(back, ('x', 'z'), split_axis=0, concat_axis=0, tiled=True)  10.2 us
    ppermute x3, starting transfers between devices, body(): lax.ppermute(across, 'x', along_x(t))  9.33 us
    pallas_call x1, Pallas kernels, label_blocks(): pl.pallas_call(block_kernel, grid=(pairs,), in_specs=[pl.BlockSpec(memory...  9.24 us
  transfers between devices with their start and end apart: 21, of which 12 were waited for; matrix products, arithmetic and copies ran while one was open for 1% of the time, Pallas kernels for 7%

profile of v2, /device:TPU:1, one launch (start us, length us, event | category | flops | bytes accessed | tf_op | source)
XLA Modules:
  0.0 184.6 jit_solution(17587685764428873809)
XLA Ops:
  2.7 11.0 %all-to-all-start = ((bf16[8,528,128]{2,1,0:T(8,128)(2,1)}), bf16[8,528,128]{2,1,0:T(8,128)(2,1)S(1)}, u32[]{:S(2)}, u32[]{:S(2)}) async-start(bf16[8,528,128]{2,1,0:T(8,128)(2,1)} %get-tuple-element.22), calls=%async_computation | async-start | bytes 2162688 | tf_op jit(solution)/shard_map/all_to_all | solution.py:432
  13.7 4.4 %collective-permute-start.2 = (bf16[272,128]{1,0:T(8,128)(2,1)S(1)}, bf16[272,128]{1,0:T(8,128)(2,1)S(1)}, u32[]{:S(2)}, u32[]{:S(2)}) collective-permute-start(bf16[272,128]{1,0:T(8,128)(2,1)S(1)} %copy-done.9), channel_id=1, source_target_pairs={{0,24},{8,0},{16,8},{24,16},{1,25},{9,1},{17,9},{25,17},{2,26},{10... | collective-permute-start | bytes 208904 | tf_op jit(solution)/shard_map/ppermute | solution.py:433
  30.9 12.7 %all-to-all-done.arrived_ref = bf16[8,528,128]{2,1,0:T(8,128)(2,1)S(1)} async-done(((bf16[8,528,128]{2,1,0:T(8,128)(2,1)}), bf16[8,528,128]{2,1,0:T(8,128)(2,1)S(1)}, u32[]{:S(2)}, u32[]{:S(2)}) %all-to-all-start) | async-done | bytes 1081376 | tf_op jit(solution)/shard_map/all_to_all | solution.py:432
  43.6 3.7 %all-to-all-start.1 = ((bf16[8,4,128,128]{3,2,1,0:T(8,128)(2,1)}), bf16[8,4,128,128]{3,2,1,0:T(8,128)(2,1)S(1)}, u32[]{:S(2)}, u32[]{:S(2)}) async-start(bf16[8,4,128,128]{3,2,1,0:T(8,128)(2,1)} %get-tuple-element.27), calls=%async_computation.1 | async-start | bytes 2097152 | tf_op jit(solution)/shard_map/all_to_all | solution.py:437
  47.3 3.4 %select_up.1 = (bf16[8,264,128]{2,1,0:T(8,128)(2,1)}, bf16[8,264,128]{2,1,0:T(8,128)(2,1)}, bf16[8,264,128]{2,1,0:T(8,128)(2,1)}, bf16[8,264,128]{2,1,0:T(8,128)(2,1)}) custom-call(s32[4]{0:T(128)} %pad_add_fusion.where_ref, bf16[8,528,128]{2,1,0:T(8,128)(2,1)} %copy-done.4), custom_call_target="tpu_custom_call" | custom-call | flops 300000000 | bytes 3000000 | tf_op jit(solution)/shard_map/select_up/pallas_call | solution.py:159
  50.7 3.1 %collective-permute-start.3 = (bf16[8,264,128]{2,1,0:T(8,128)(2,1)}, bf16[8,264,128]{2,1,0:T(8,128)(2,1)S(1)}, u32[]{:S(2)}, u32[]{:S(2)}) collective-permute-start(bf16[8,264,128]{2,1,0:T(8,128)(2,1)} %get-tuple-element.24), channel_id=1, source_target_pairs={{0,8},{8,16},{16,24},{24,0},{1,9},{9,17},{17,25},{25,1},{2,10},{10... | collective-permute-start | bytes 1622024 | tf_op jit(solution)/shard_map/ppermute | solution.py:438
  53.8 4.4 %collective-permute-start.4 = (bf16[8,264,128]{2,1,0:T(8,128)(2,1)}, bf16[8,264,128]{2,1,0:T(8,128)(2,1)S(1)}, u32[]{:S(2)}, u32[]{:S(2)}) collective-permute-start(bf16[8,264,128]{2,1,0:T(8,128)(2,1)} %get-tuple-element.25), channel_id=1, source_target_pairs={{0,16},{8,24},{16,0},{24,8},{1,17},{9,25},{17,1},{25,9},{2,18},{10... | collective-permute-start | bytes 1622024 | tf_op jit(solution)/shard_map/ppermute | solution.py:436
  58.2 3.1 %collective-permute-start.5 = (bf16[8,264,128]{2,1,0:T(8,128)(2,1)}, bf16[8,264,128]{2,1,0:T(8,128)(2,1)S(1)}, u32[]{:S(2)}, u32[]{:S(2)}) collective-permute-start(bf16[8,264,128]{2,1,0:T(8,128)(2,1)} %get-tuple-element.26), channel_id=1, source_target_pairs={{0,24},{8,0},{16,8},{24,16},{1,25},{9,1},{17,9},{25,17},{2,26},{10... | collective-permute-start | bytes 1622024 | tf_op jit(solution)/shard_map/ppermute | solution.py:438
  61.2 15.2 %all-to-all-done.1.b_ref = bf16[8,4,128,128]{3,2,1,0:T(8,128)(2,1)S(1)} async-done(((bf16[8,4,128,128]{3,2,1,0:T(8,128)(2,1)}), bf16[8,4,128,128]{3,2,1,0:T(8,128)(2,1)S(1)}, u32[]{:S(2)}, u32[]{:S(2)}) %all-to-all-start.1) | async-done | bytes 1048608 | tf_op jit(solution)/shard_map/all_to_all | solution.py:437
  76.5 3.4 %collective-permute-done.4.a2_ref = bf16[8,264,128]{2,1,0:T(8,128)(2,1)S(1)} collective-permute-done((bf16[8,264,128]{2,1,0:T(8,128)(2,1)}, bf16[8,264,128]{2,1,0:T(8,128)(2,1)S(1)}, u32[]{:S(2)}, u32[]{:S(2)}) %collective-permute-start.4) | collective-permute-done | bytes 540704 | tf_op jit(solution)/shard_map/ppermute | solution.py:436
  82.4 9.2 %label_blocks.1 = (bf16[32,6,4,16,128]{4,3,2,1,0:T(8,128)(2,1)}, f32[8,64,768]{2,1,0:T(8,128)}, f32[8,64,768]{2,1,0:T(8,128)}) custom-call(s32[4]{0:T(128)S(1)} %copy-done.2, bf16[8,264,128]{2,1,0:T(8,128)(2,1)S(1)} %copy-done.1, bf16[8,264,128]{2,1,0:T(8,128)(2,1)S(1)} %collective-permute-done.3.a1_ref, ...), custom_call_target="tpu_custom_call" | custom-call | flops 1210000000 | bytes 11000000 | tf_op jit(solution)/shard_map/label_blocks/pallas_call | solution.py:239
  91.6 10.2 %all-to-all-start.2 = ((bf16[32,384,128]{2,1,0:T(8,128)(2,1)}), bf16[32,384,128]{2,1,0:T(8,128)(2,1)}, u32[]{:S(2)}, u32[]{:S(2)}) async-start(bf16[32,384,128]{2,1,0:T(8,128)(2,1)} %bitcast.17), calls=%async_computation.2 | async-start | bytes 6291456 | tf_op jit(solution)/shard_map/all_to_all | solution.py:442
  101.9 3.0 %collective-permute-start.6 = (f32[8,64,768]{2,1,0:T(8,128)S(1)}, f32[8,64,768]{2,1,0:T(8,128)S(1)}, u32[]{:S(2)}, u32[]{:S(2)}) collective-permute-start(f32[8,64,768]{2,1,0:T(8,128)S(1)} %copy-done.8), channel_id=1, source_target_pairs={{0,32},{32,0},{64,96},{96,64},{128,160},{160,128},{192,224},{224,1... | collective-permute-start | bytes 4718600 | tf_op jit(solution)/shard_map/ppermute | solution.py:443
  111.9 5.2 %collective-permute-start.7 = (bf16[128,768]{1,0:T(8,128)(2,1)}, bf16[128,768]{1,0:T(8,128)(2,1)S(1)}, u32[]{:S(2)}, u32[]{:S(2)}) collective-permute-start(bf16[128,768]{1,0:T(8,128)(2,1)} %get-tuple-element.32), channel_id=1, source_target_pairs={{0,64},{32,480},{64,128},{96,32},{128,192},{160,96},{192,256},{224... | collective-permute-start | bytes 589832 | tf_op jit(solution)/shard_map/ppermute | solution.py:447
  117.2 3.8 %collective-permute-start.8 = (bf16[128,768]{1,0:T(8,128)(2,1)}, bf16[128,768]{1,0:T(8,128)(2,1)S(1)}, u32[]{:S(2)}, u32[]{:S(2)}) collective-permute-start(bf16[128,768]{1,0:T(8,128)(2,1)} %get-tuple-element.33), channel_id=1, source_target_pairs={{0,128},{32,416},{64,192},{96,480},{128,256},{160,32},{192,320},{2... | collective-permute-start | bytes 589832 | tf_op jit(solution)/shard_map/ppermute | solution.py:447
  123.7 5.7 %collective-permute-start.10 = (bf16[64,768]{1,0:T(8,128)(2,1)}, bf16[64,768]{1,0:T(8,128)(2,1)S(1)}, u32[]{:S(2)}, u32[]{:S(2)}) collective-permute-start(bf16[64,768]{1,0:T(8,128)(2,1)} %get-tuple-element.35), channel_id=1, source_target_pairs={{0,256},{32,288},{64,320},{96,352},{128,384},{160,416},{192,448},{... | collective-permute-start | bytes 294920 | tf_op jit(solution)/shard_map/ppermute | solution.py:449
  130.2 5.8 %collective-permute-done.10 = bf16[64,768]{1,0:T(8,128)(2,1)S(1)} collective-permute-done((bf16[64,768]{1,0:T(8,128)(2,1)}, bf16[64,768]{1,0:T(8,128)(2,1)S(1)}, u32[]{:S(2)}, u32[]{:S(2)}) %collective-permute-start.10) | collective-permute-done | bytes 98336 | tf_op jit(solution)/shard_map/ppermute | solution.py:449
  136.1 4.4 %collective-permute-start.11 = (f32[64,768]{1,0:T(8,128)S(1)}, f32[64,768]{1,0:T(8,128)S(1)}, u32[]{:S(2)}, u32[]{:S(2)}) collective-permute-start(f32[64,768]{1,0:T(8,128)S(1)} %fusion.4), channel_id=1, source_target_pairs={{0,32},{32,0},{64,96},{96,64},{128,160},{160,128},{192,224},{224,1... | collective-permute-start | bytes 589832 | tf_op jit(solution)/shard_map/ppermute | solution.py:453
  145.9 5.0 %collective-permute-start.16 = (bf16[128,768]{1,0:T(8,128)(2,1)S(1)}, bf16[128,768]{1,0:T(8,128)(2,1)S(1)}, u32[]{:S(2)}, u32[]{:S(2)}) collective-permute-start(bf16[128,768]{1,0:T(8,128)(2,1)S(1)} %pad_maximum_fusion.1.both_ref), channel_id=1, source_target_pairs={{0,192},{32,352},{64,256},{96,416},{128,320},{160,480},{192,384},{... | collective-permute-start | bytes 589832 | tf_op jit(solution)/shard_map/ppermute | solution.py:465
  150.9 3.4 %collective-permute-start.15 = (bf16[128,768]{1,0:T(8,128)(2,1)S(1)}, bf16[128,768]{1,0:T(8,128)(2,1)S(1)}, u32[]{:S(2)}, u32[]{:S(2)}) collective-permute-start(bf16[128,768]{1,0:T(8,128)(2,1)S(1)} %pad_maximum_fusion.1.both_ref), channel_id=1, source_target_pairs={{0,128},{32,416},{64,192},{96,480},{128,256},{160,32},{192,320},{2... | collective-permute-start | bytes 589832 | tf_op jit(solution)/shard_map/ppermute | solution.py:465
  154.3 4.3 %collective-permute-start.14 = (bf16[128,768]{1,0:T(8,128)(2,1)S(1)}, bf16[128,768]{1,0:T(8,128)(2,1)S(1)}, u32[]{:S(2)}, u32[]{:S(2)}) collective-permute-start(bf16[128,768]{1,0:T(8,128)(2,1)S(1)} %pad_maximum_fusion.1.both_ref), channel_id=1, source_target_pairs={{0,64},{32,480},{64,128},{96,32},{128,192},{160,96},{192,256},{224... | collective-permute-start | bytes 589832 | tf_op jit(solution)/shard_map/ppermute | solution.py:465
  158.6 5.1 %collective-permute-start.12 = (bf16[64,768]{1,0:T(8,128)(2,1)S(1)}, bf16[64,768]{1,0:T(8,128)(2,1)S(1)}, u32[]{:S(2)}, u32[]{:S(2)}) collective-permute-start(bf16[64,768]{1,0:T(8,128)(2,1)S(1)} %get-tuple-element.36), channel_id=1, source_target_pairs={{0,256},{32,288},{64,320},{96,352},{128,384},{160,416},{192,448},{... | collective-permute-start | bytes 294920 | tf_op jit(solution)/shard_map/ppermute | solution.py:460
  163.7 9.1 %collective-permute-done.12.mine_ref = bf16[64,768]{1,0:T(8,128)(2,1)S(1)} collective-permute-done((bf16[64,768]{1,0:T(8,128)(2,1)S(1)}, bf16[64,768]{1,0:T(8,128)(2,1)S(1)}, u32[]{:S(2)}, u32[]{:S(2)}) %collective-permute-start.12) | collective-permute-done | bytes 98336 | tf_op jit(solution)/shard_map/ppermute | solution.py:460
  180.3 4.2 %sum_parts.1 = f32[128,768]{1,0:T(8,128)} custom-call(bf16[2048,128]{1,0:T(8,128)(2,1)} %get-tuple-element.21.pick_ref, bf16[32,384,128]{2,1,0:T(8,128)(2,1)} %all-to-all-done.2.back_ref), custom_call_target="tpu_custom_call" | custom-call | flops 400000000 | bytes 4000000 | tf_op jit(solution)/shard_map/sum_parts/pallas_call | solution.py:295
  (59 shorter events, 40.8 us)
Async XLA Ops:
  2.7 40.9 %all-to-all-start = ((bf16[8,528,128]{2,1,0:T(8,128)(2,1)}), bf16[8,528,128]{2,1,0:T(8,128)(2,1)S(1)}, u32[]{:S(2)}, u32[]{:S(2)}) async-start(bf16[8,528,128]{2,1,0:T(8,128)(2,1)} %get-tuple-element.22), calls=%async_computation | async-start | bytes 2162688 | tf_op jit(solution)/shard_map/all_to_all | solution.py:432
  13.7 10.0 %collective-permute-start.2 = (bf16[272,128]{1,0:T(8,128)(2,1)S(1)}, bf16[272,128]{1,0:T(8,128)(2,1)S(1)}, u32[]{:S(2)}, u32[]{:S(2)}) collective-permute-start(bf16[272,128]{1,0:T(8,128)(2,1)S(1)} %copy-done.9), channel_id=1, source_target_pairs={{0,24},{8,0},{16,8},{24,16},{1,25},{9,1},{17,9},{25,17},{2,26},{10... | collective-permute-start | bytes 208904 | tf_op jit(solution)/shard_map/ppermute | solution.py:433
  18.1 6.9 %collective-permute-start.1 = (bf16[272,128]{1,0:T(8,128)(2,1)S(1)}, bf16[272,128]{1,0:T(8,128)(2,1)S(1)}, u32[]{:S(2)}, u32[]{:S(2)}) collective-permute-start(bf16[272,128]{1,0:T(8,128)(2,1)S(1)} %copy-done.9), channel_id=1, source_target_pairs={{0,16},{8,24},{16,0},{24,8},{1,17},{9,25},{17,1},{25,9},{2,18},{10... | collective-permute-start | bytes 208904 | tf_op jit(solution)/shard_map/ppermute | solution.py:433
  20.5 7.0 %collective-permute-start = (bf16[272,128]{1,0:T(8,128)(2,1)S(1)}, bf16[272,128]{1,0:T(8,128)(2,1)S(1)}, u32[]{:S(2)}, u32[]{:S(2)}) collective-permute-start(bf16[272,128]{1,0:T(8,128)(2,1)S(1)} %copy-done.9), channel_id=1, source_target_pairs={{0,8},{8,16},{16,24},{24,0},{1,9},{9,17},{17,25},{25,1},{2,10},{10... | collective-permute-start | bytes 208904 | tf_op jit(solution)/shard_map/ppermute | solution.py:433
  43.6 37.7 %copy-start.2 = (s32[4]{0:T(128)S(1)}, s32[4]{0:T(128)}, u32[]{:S(2)}) copy-start(s32[4]{0:T(128)} %pad_add_fusion.where_ref) | copy-start | bytes 52
  43.6 32.9 %all-to-all-start.1 = ((bf16[8,4,128,128]{3,2,1,0:T(8,128)(2,1)}), bf16[8,4,128,128]{3,2,1,0:T(8,128)(2,1)S(1)}, u32[]{:S(2)}, u32[]{:S(2)}) async-start(bf16[8,4,128,128]{3,2,1,0:T(8,128)(2,1)} %get-tuple-element.27), calls=%async_computation.1 | async-start | bytes 2097152 | tf_op jit(solution)/shard_map/all_to_all | solution.py:437
  50.7 25.8 %collective-permute-start.3 = (bf16[8,264,128]{2,1,0:T(8,128)(2,1)}, bf16[8,264,128]{2,1,0:T(8,128)(2,1)S(1)}, u32[]{:S(2)}, u32[]{:S(2)}) collective-permute-start(bf16[8,264,128]{2,1,0:T(8,128)(2,1)} %get-tuple-element.24), channel_id=1, source_target_pairs={{0,8},{8,16},{16,24},{24,0},{1,9},{9,17},{17,25},{25,1},{2,10},{10... | collective-permute-start | bytes 1622024 | tf_op jit(solution)/shard_map/ppermute | solution.py:438
  53.8 26.1 %collective-permute-start.4 = (bf16[8,264,128]{2,1,0:T(8,128)(2,1)}, bf16[8,264,128]{2,1,0:T(8,128)(2,1)S(1)}, u32[]{:S(2)}, u32[]{:S(2)}) collective-permute-start(bf16[8,264,128]{2,1,0:T(8,128)(2,1)} %get-tuple-element.25), channel_id=1, source_target_pairs={{0,16},{8,24},{16,0},{24,8},{1,17},{9,25},{17,1},{25,9},{2,18},{10... | collective-permute-start | bytes 1622024 | tf_op jit(solution)/shard_map/ppermute | solution.py:436
  58.2 23.2 %collective-permute-start.5 = (bf16[8,264,128]{2,1,0:T(8,128)(2,1)}, bf16[8,264,128]{2,1,0:T(8,128)(2,1)S(1)}, u32[]{:S(2)}, u32[]{:S(2)}) collective-permute-start(bf16[8,264,128]{2,1,0:T(8,128)(2,1)} %get-tuple-element.26), channel_id=1, source_target_pairs={{0,24},{8,0},{16,8},{24,16},{1,25},{9,1},{17,9},{25,17},{2,26},{10... | collective-permute-start | bytes 1622024 | tf_op jit(solution)/shard_map/ppermute | solution.py:438
  91.6 88.7 %all-to-all-start.2 = ((bf16[32,384,128]{2,1,0:T(8,128)(2,1)}), bf16[32,384,128]{2,1,0:T(8,128)(2,1)}, u32[]{:S(2)}, u32[]{:S(2)}) async-start(bf16[32,384,128]{2,1,0:T(8,128)(2,1)} %bitcast.17), calls=%async_computation.2 | async-start | bytes 6291456 | tf_op jit(solution)/shard_map/all_to_all | solution.py:442
  101.9 6.1 %collective-permute-start.6 = (f32[8,64,768]{2,1,0:T(8,128)S(1)}, f32[8,64,768]{2,1,0:T(8,128)S(1)}, u32[]{:S(2)}, u32[]{:S(2)}) collective-permute-start(f32[8,64,768]{2,1,0:T(8,128)S(1)} %copy-done.8), channel_id=1, source_target_pairs={{0,32},{32,0},{64,96},{96,64},{128,160},{160,128},{192,224},{224,1... | collective-permute-start | bytes 4718600 | tf_op jit(solution)/shard_map/ppermute | solution.py:443
  111.9 29.7 %copy-start.7 = (f32[64,768]{1,0:T(8,128)S(1)}, f32[64,768]{1,0:T(8,128)}, u32[]{:S(2)}) copy-start(f32[64,768]{1,0:T(8,128)} %get-tuple-element.31) | copy-start | bytes 589828
  111.9 17.4 %collective-permute-start.7 = (bf16[128,768]{1,0:T(8,128)(2,1)}, bf16[128,768]{1,0:T(8,128)(2,1)S(1)}, u32[]{:S(2)}, u32[]{:S(2)}) collective-permute-start(bf16[128,768]{1,0:T(8,128)(2,1)} %get-tuple-element.32), channel_id=1, source_target_pairs={{0,64},{32,480},{64,128},{96,32},{128,192},{160,96},{192,256},{224... | collective-permute-start | bytes 589832 | tf_op jit(solution)/shard_map/ppermute | solution.py:447
  117.2 12.2 %collective-permute-start.8 = (bf16[128,768]{1,0:T(8,128)(2,1)}, bf16[128,768]{1,0:T(8,128)(2,1)S(1)}, u32[]{:S(2)}, u32[]{:S(2)}) collective-permute-start(bf16[128,768]{1,0:T(8,128)(2,1)} %get-tuple-element.33), channel_id=1, source_target_pairs={{0,128},{32,416},{64,192},{96,480},{128,256},{160,32},{192,320},{2... | collective-permute-start | bytes 589832 | tf_op jit(solution)/shard_map/ppermute | solution.py:447
  120.9 9.2 %collective-permute-start.9 = (bf16[128,768]{1,0:T(8,128)(2,1)}, bf16[128,768]{1,0:T(8,128)(2,1)S(1)}, u32[]{:S(2)}, u32[]{:S(2)}) collective-permute-start(bf16[128,768]{1,0:T(8,128)(2,1)} %get-tuple-element.34), channel_id=1, source_target_pairs={{0,192},{32,352},{64,256},{96,416},{128,320},{160,480},{192,384},{... | collective-permute-start | bytes 589832 | tf_op jit(solution)/shard_map/ppermute | solution.py:447
  123.7 12.4 %collective-permute-start.10 = (bf16[64,768]{1,0:T(8,128)(2,1)}, bf16[64,768]{1,0:T(8,128)(2,1)S(1)}, u32[]{:S(2)}, u32[]{:S(2)}) collective-permute-start(bf16[64,768]{1,0:T(8,128)(2,1)} %get-tuple-element.35), channel_id=1, source_target_pairs={{0,256},{32,288},{64,320},{96,352},{128,384},{160,416},{192,448},{... | collective-permute-start | bytes 294920 | tf_op jit(solution)/shard_map/ppermute | solution.py:449
  136.1 5.5 %collective-permute-start.11 = (f32[64,768]{1,0:T(8,128)S(1)}, f32[64,768]{1,0:T(8,128)S(1)}, u32[]{:S(2)}, u32[]{:S(2)}) collective-permute-start(f32[64,768]{1,0:T(8,128)S(1)} %fusion.4), channel_id=1, source_target_pairs={{0,32},{32,0},{64,96},{96,64},{128,160},{160,128},{192,224},{224,1... | collective-permute-start | bytes 589832 | tf_op jit(solution)/shard_map/ppermute | solution.py:453
  142.5 33.1 %copy-start = (bf16[1024,768]{1,0:T(8,128)(2,1)S(1)}, bf16[1024,768]{1,0:T(8,128)(2,1)}, u32[]{:S(2)}) copy-start(bf16[1024,768]{1,0:T(8,128)(2,1)} %tile_ref.3) | copy-start | bytes 4718596
  142.5 3.3 %collective-permute-start.13 = (bf16[64,768]{1,0:T(8,128)(2,1)S(1)}, bf16[64,768]{1,0:T(8,128)(2,1)S(1)}, u32[]{:S(2)}, u32[]{:S(2)}) collective-permute-start(bf16[64,768]{1,0:T(8,128)(2,1)S(1)} %get-tuple-element.36), channel_id=1, source_target_pairs={{0,32},{32,0},{64,96},{96,64},{128,160},{160,128},{192,224},{224,1... | collective-permute-start | bytes 294920 | tf_op jit(solution)/shard_map/ppermute | solution.py:461
  145.9 27.0 %collective-permute-start.16 = (bf16[128,768]{1,0:T(8,128)(2,1)S(1)}, bf16[128,768]{1,0:T(8,128)(2,1)S(1)}, u32[]{:S(2)}, u32[]{:S(2)}) collective-permute-start(bf16[128,768]{1,0:T(8,128)(2,1)S(1)} %pad_maximum_fusion.1.both_ref), channel_id=1, source_target_pairs={{0,192},{32,352},{64,256},{96,416},{128,320},{160,480},{192,384},{... | collective-permute-start | bytes 589832 | tf_op jit(solution)/shard_map/ppermute | solution.py:465
  150.9 22.0 %collective-permute-start.15 = (bf16[128,768]{1,0:T(8,128)(2,1)S(1)}, bf16[128,768]{1,0:T(8,128)(2,1)S(1)}, u32[]{:S(2)}, u32[]{:S(2)}) collective-permute-start(bf16[128,768]{1,0:T(8,128)(2,1)S(1)} %pad_maximum_fusion.1.both_ref), channel_id=1, source_target_pairs={{0,128},{32,416},{64,192},{96,480},{128,256},{160,32},{192,320},{2... | collective-permute-start | bytes 589832 | tf_op jit(solution)/shard_map/ppermute | solution.py:465
  154.3 18.6 %collective-permute-start.14 = (bf16[128,768]{1,0:T(8,128)(2,1)S(1)}, bf16[128,768]{1,0:T(8,128)(2,1)S(1)}, u32[]{:S(2)}, u32[]{:S(2)}) collective-permute-start(bf16[128,768]{1,0:T(8,128)(2,1)S(1)} %pad_maximum_fusion.1.both_ref), channel_id=1, source_target_pairs={{0,64},{32,480},{64,128},{96,32},{128,192},{160,96},{192,256},{224... | collective-permute-start | bytes 589832 | tf_op jit(solution)/shard_map/ppermute | solution.py:465
  158.6 14.3 %collective-permute-start.12 = (bf16[64,768]{1,0:T(8,128)(2,1)S(1)}, bf16[64,768]{1,0:T(8,128)(2,1)S(1)}, u32[]{:S(2)}, u32[]{:S(2)}) collective-permute-start(bf16[64,768]{1,0:T(8,128)(2,1)S(1)} %get-tuple-element.36), channel_id=1, source_target_pairs={{0,256},{32,288},{64,320},{96,352},{128,384},{160,416},{192,448},{... | collective-permute-start | bytes 294920 | tf_op jit(solution)/shard_map/ppermute | solution.py:460
  172.9 5.0 %collective-permute-start.17 = (bf16[448,768]{1,0:T(8,128)(2,1)S(1)}, bf16[448,768]{1,0:T(8,128)(2,1)S(1)}, u32[]{:S(2)}, u32[]{:S(2)}) collective-permute-start(bf16[448,768]{1,0:T(8,128)(2,1)S(1)} %pad_maximum_fusion), channel_id=1, source_target_pairs={{0,32},{32,0},{64,96},{96,64},{128,160},{160,128},{192,224},{224,1... | collective-permute-start | bytes 2064392 | tf_op jit(solution)/shard_map/ppermute | solution.py:466
  (10 other events, 93.4 us)
